TPU v7x, 32 devices: a whole 2x2x4 slice. The times are simulated.
32 devices in a mesh: ctx: 16 (over z, y, core), wsh: 2 (over x).
Axes of the slice: x: 2, y: 2, z: 4, core: 2. Of those that a mesh axis runs over, the one named last changes fastest.
Arguments:
- tokens: bfloat16 [4, 2048, 1024], P('wsh', 'ctx'), may hold values from -6 to 6
- segment_ids: int32 [4, 2048], P('wsh', 'ctx'), may hold values from 0 to 15, never falling along the last dimension, each value on 1 to 512 neighbouring positions
- cotangent: bfloat16 [4, 2048, 1024], P('wsh', 'ctx'), may hold values from -6 to 6
- qkv_master: float32 [1024, 2048], P('wsh', 'ctx'), may hold values from -0.1875 to 0.1875
- qkv_mean: float32 [1024, 2048], P('wsh', 'ctx'), may hold values from -27.1529 to 27.1529
- qkv_square: float32 [1024, 2048], P('wsh', 'ctx'), may hold values from 0.8192 to 13.1072
- proj_master: float32 [1024, 1024], P('wsh', 'ctx'), may hold values from -1.5 to 1.5
- proj_mean: float32 [1024, 1024], P('wsh', 'ctx'), may hold values from -27.1529 to 27.1529
- proj_square: float32 [1024, 1024], P('wsh', 'ctx'), may hold values from 0.8192 to 13.1072
- upgate_master: float32 [1024, 9216], P('wsh', 'ctx'), may hold values from -0.1875 to 0.1875
- upgate_mean: float32 [1024, 9216], P('wsh', 'ctx'), may hold values from -27.1529 to 27.1529
- upgate_square: float32 [1024, 9216], P('wsh', 'ctx'), may hold values from 0.8192 to 13.1072
- down_master: float32 [4608, 1024], P('wsh', 'ctx'), may hold values from -0.09375 to 0.09375
- down_mean: float32 [4608, 1024], P('wsh', 'ctx'), may hold values from -27.1529 to 27.1529
- down_square: float32 [4608, 1024], P('wsh', 'ctx'), may hold values from 0.8192 to 13.1072
- gain_master: float32 [2176], replicated, may hold values from 0.5 to 1.5
- gain_mean: float32 [2176], replicated, may hold values from -27.1529 to 27.1529
- gain_square: float32 [2176], replicated, may hold values from 0.8192 to 13.1072
Outputs:
- block_out: bfloat16 [4, 2048, 1024], P('wsh', 'ctx')
- input_grad: float32 [4, 2048, 1024], P('wsh', 'ctx')
- qkv_grad: float32 [1024, 2048], P('wsh', 'ctx')
- qkv_weight: float32 [1024, 2048], P('wsh', 'ctx')
- qkv_first: float32 [1024, 2048], P('wsh', 'ctx')
- qkv_second: float32 [1024, 2048], P('wsh', 'ctx')
- proj_grad: float32 [1024, 1024], P('wsh', 'ctx')
- proj_weight: float32 [1024, 1024], P('wsh', 'ctx')
- proj_first: float32 [1024, 1024], P('wsh', 'ctx')
- proj_second: float32 [1024, 1024], P('wsh', 'ctx')
- upgate_grad: float32 [1024, 9216], P('wsh', 'ctx')
- upgate_weight: float32 [1024, 9216], P('wsh', 'ctx')
- upgate_first: float32 [1024, 9216], P('wsh', 'ctx')
- upgate_second: float32 [1024, 9216], P('wsh', 'ctx')
- down_grad: float32 [4608, 1024], P('wsh', 'ctx')
- down_weight: float32 [4608, 1024], P('wsh', 'ctx')
- down_first: float32 [4608, 1024], P('wsh', 'ctx')
- down_second: float32 [4608, 1024], P('wsh', 'ctx')
- gain_grad: float32 [2176], replicated
- gain_weight: float32 [2176], replicated
- gain_first: float32 [2176], replicated
- gain_second: float32 [2176], replicated
- lamb_norms: float32 [2, 8], replicated
Inputs may be any that keep to these rules, and one draw needn't show every extreme that they name: `segment_ids`: in each sequence the numbers never fall; a sequence holds 16 documents of 1 to 512 tokens, one of exactly 512 tokens.
All inputs are finite; a program needn't handle non-finite values.
Results may differ from a plain program's by a relative error of at most 0.02.
Values may be sent and summed in bfloat16 or wider, within the bound.
No kernel may reach another device: no remote copies, remote signals or barrier semaphores. Data moves between devices by JAX's collectives and lax.ppermute only.
A program may use at most 192 MiB of HBM per device.

v0:
```python
import functools

import jax
import jax.numpy as jnp
from jax import lax
from jax.experimental import pallas as pl
from jax.experimental.pallas import tpu as pltpu
from jax.sharding import Mesh
from jax.sharding import PartitionSpec as P


D = 1024
QUERY_HEADS = 16
KEY_VALUE_HEADS = 8
HEAD_WIDTH = 64
STEP = 10
GAINS = 2176
QUERY_COLUMNS = QUERY_HEADS * HEAD_WIDTH
KEY_COLUMNS = KEY_VALUE_HEADS * HEAD_WIDTH
PAIR = 2 * HEAD_WIDTH
N_PAIRS = KEY_VALUE_HEADS // 2

EPS_NORM = 1e-05
BETA_ONE = 0.9
BETA_TWO = 0.999
EPS_ADAM = 1e-06
DECAY = 0.01
RATE = 0.5
NEGATIVE_FILLER = -1e30

FAR = ("hi", "top", "low")
CTX = (*FAR, "near", "core")
QUARTERS = ("hi", "top")
EVERY = (*CTX, "wsh")
OTHERS = ("hi", "wsh", "low", "near")

BF = jnp.bfloat16
F32 = jnp.float32


def swap(block, axis):
    return lax.ppermute(block, axis, [(0, 1), (1, 0)])


def from_earlier(package, depth):
    here, quarter, n, k = (lax.axis_index(a) for a in (CTX, QUARTERS, "near", "core"))
    if lax.axis_size("low") > 1:
        size = lax.axis_size(CTX)
        blocks, exists = [], []
        for distance in range(1, depth + 1):
            route = [(i - distance, i) for i in range(distance, size)]
            blocks.append(lax.ppermute(package, CTX, route))
            exists.append(here >= distance)
        return blocks, exists
    before = lax.ppermute(package, QUARTERS, [(0, 1), (1, 2), (2, 3)])
    across = swap(jnp.where(n == 0, package, before), "near")
    beside = swap(jnp.where(k == 0, package, before), "core")
    diagonal = swap(across, "core")
    later = quarter > 0
    return [before, across, beside, diagonal], [later, later | (n == 1), later | (k == 1), later | (n == 1)]


def to_earlier(parts, own):
    n, k = lax.axis_index("near"), lax.axis_index("core")
    if lax.axis_size("low") > 1:
        size = lax.axis_size(CTX)
        for distance, part in enumerate(parts, 1):
            route = [(i, i - distance) for i in range(distance, size)]
            own = own + lax.ppermute(part, CTX, route).astype(F32)
        return own
    before, across, beside, diagonal = parts
    beside = swap(beside, "core").astype(F32)
    diagonal = swap(diagonal, "core").astype(F32)
    across = swap((across.astype(F32) + diagonal).astype(BF), "near").astype(F32)
    before = before.astype(F32) + jnp.where(k == 1, beside, 0.0) + jnp.where(n == 1, across, 0.0)
    after = lax.ppermute(before.astype(BF), QUARTERS, [(1, 0), (2, 1), (3, 2)]).astype(F32)
    return own + jnp.where(k == 0, beside, 0.0) + jnp.where(n == 0, across, 0.0) + after


def in_order(mine, other, index, at=0):
    return jnp.where(index == 0, jnp.stack([mine, other], at), jnp.stack([other, mine], at))


def pick(array, index, axis):
    return lax.dynamic_index_in_dim(array, index, axis, keepdims=False)


def total_everywhere(block):
    for axis in ("core", "wsh", "near", "hi", "top", "low"):
        size = lax.axis_size(axis)
        step = 1
        while step < size:
            block = block + lax.ppermute(block, axis, [(i, i ^ step) for i in range(size)])
            step *= 2
    return block


def rms_norm(inputs, gain):
    inverse = lax.rsqrt(jnp.mean(inputs * inputs, axis=-1, keepdims=True) + EPS_NORM)
    return inputs * inverse * gain, inverse


def norm_back(inputs, inverse, gain, grad_out):
    weighted = grad_out * gain
    inner = jnp.mean(weighted * inputs, axis=-1, keepdims=True)
    grad_in = inverse * weighted - inputs * (inverse * inverse * inverse) * inner
    return grad_in, grad_out * inputs * inverse


def lamb_moments(grad, mean, square):
    first = BETA_ONE * mean + (1.0 - BETA_ONE) * grad
    second = BETA_TWO * square + (1.0 - BETA_TWO) * grad * grad
    bias_one = 1.0 - BETA_ONE**STEP
    bias_two = 1.0 - BETA_TWO**STEP
    direction = first / bias_one / (jnp.sqrt(second / bias_two) + EPS_ADAM)
    return first, second, direction


def low_half():
    return lax.broadcasted_iota(jnp.int32, (1, PAIR), 1) < HEAD_WIDTH


def dot_nt(a, b):
    return lax.dot_general(a, b, (((1,), (1,)), ((), ())), preferred_element_type=F32)


def dot_tn(a, b):
    return lax.dot_general(a, b, (((0,), (0,)), ((), ())), preferred_element_type=F32)


def dot_nn(a, b):
    return lax.dot_general(a, b, (((1,), (0,)), ((), ())), preferred_element_type=F32)


def half_sums(block):
    row = lax.broadcasted_iota(jnp.int32, (PAIR, PAIR), 0) < HEAD_WIDTH
    col = lax.broadcasted_iota(jnp.int32, (PAIR, PAIR), 1) < HEAD_WIDTH
    ones = jnp.where(row == col, 1.0, 0.0).astype(BF)
    high = block.astype(BF)
    rest = (block - high.astype(F32)).astype(BF)
    return dot_nn(high, ones) + dot_nn(rest, ones)


def head_norm(block, gain):
    inverse = lax.rsqrt(half_sums(block * block) * (1.0 / HEAD_WIDTH) + EPS_NORM)
    return block * inverse * gain, inverse


def head_norm_back(raw, inverse, gain, grad):
    weighted = grad * gain
    inner = half_sums(weighted * raw) * (1.0 / HEAD_WIDTH)
    return inverse * weighted - raw * (inverse * inverse * inverse) * inner


def spread(block):
    low = low_half()
    turned = pltpu.roll(block, HEAD_WIDTH, 1)
    return jnp.where(low, block, turned).astype(BF), jnp.where(low, turned, block).astype(BF)


def stacked(block):
    low = low_half()
    return jnp.concatenate([jnp.where(low, block, 0.0), jnp.where(low, 0.0, block)], axis=0).astype(BF)


def unstacked(block):
    rows = block.shape[0] // 2
    return jnp.where(low_half(), block[:rows], block[rows:])


def allowed_mask(q_seg, k_seg):
    rows = q_seg.shape[1]
    behind = (k_seg.shape[0] - 1) * rows
    columns = [jnp.broadcast_to(k_seg[i : i + 1], (rows, rows)).T for i in range(k_seg.shape[0])]
    k_column = jnp.concatenate(columns, axis=0)
    key = lax.broadcasted_iota(jnp.int32, k_column.shape, 0)
    query = lax.broadcasted_iota(jnp.int32, k_column.shape, 1)
    mask = (k_column == q_seg) & (key <= query + behind)
    return jnp.concatenate([mask, mask], axis=1)


def joined(ref):
    return ref[:, 0].reshape(-1, ref.shape[3])


def softmax_parts(scores, mask):
    filled = jnp.where(mask, scores, NEGATIVE_FILLER)
    top = jnp.max(filled, axis=0, keepdims=True)
    weights = jnp.exp(filled - top)
    return weights, 1.0 / jnp.sum(weights, axis=0, keepdims=True)


def forward_kernel(q_ref, k_ref, v_ref, qs_ref, ks_ref, gq_ref, gk_ref, o_ref):
    mask = allowed_mask(qs_ref[0], ks_ref[0])
    key_pair = spread(head_norm(joined(k_ref), gk_ref[...])[0])
    value_pair = spread(joined(v_ref))
    for head in range(2):
        at = pl.ds(head * PAIR, PAIR)
        query = head_norm(q_ref[0, :, at], gq_ref[...])[0].astype(BF).astype(F32)
        scores = dot_nt(key_pair[head], stacked(query * HEAD_WIDTH**-0.5))
        weights, inverse = softmax_parts(scores, mask)
        attended = dot_tn(value_pair[head], weights.astype(BF)) * inverse
        o_ref[0, :, at] = unstacked(attended.T).astype(BF)


def backward_kernel(
    q_ref, k_ref, v_ref, go_ref, qs_ref, ks_ref, gq_ref, gk_ref, gq_out, gk_out, gv_out, gain_out
):
    mask = allowed_mask(qs_ref[0], ks_ref[0])
    raw_key = joined(k_ref)
    normed_key, inverse_key = head_norm(raw_key, gk_ref[...])
    key_pair = spread(normed_key)
    value_pair = spread(joined(v_ref))
    low = low_half()
    shape = (k_ref.shape[0], *k_ref.shape[2:])

    @pl.when((pl.program_id(0) == 0) & (pl.program_id(1) == 0))
    def _():
        gain_out[...] = jnp.zeros_like(gain_out)

    grad_keys, grad_values = [], []
    for head in range(2):
        at = pl.ds(head * PAIR, PAIR)
        raw = q_ref[0, :, at]
        normed, inverse_norm = head_norm(raw, gq_ref[...])
        query = stacked(normed.astype(BF).astype(F32) * HEAD_WIDTH**-0.5)
        weights, inverse = softmax_parts(dot_nt(key_pair[head], query), mask)
        probs = weights * inverse
        grad_out = stacked(go_ref[0, :, at].astype(F32))
        grad_probs = dot_nt(value_pair[head], grad_out)
        delta = jnp.sum(probs * grad_probs, axis=0, keepdims=True)
        grad_scores = (probs * (grad_probs - delta)).astype(BF)
        grad_query = unstacked(dot_tn(key_pair[head], grad_scores).T) * HEAD_WIDTH**-0.5
        key_part = dot_nn(grad_scores, query)
        value_part = dot_nn(probs.astype(BF), grad_out)
        grad_keys.append(key_part + pltpu.roll(key_part, HEAD_WIDTH, 1))
        grad_values.append(value_part + pltpu.roll(value_part, HEAD_WIDTH, 1))
        gq_out[0, :, at] = head_norm_back(raw, inverse_norm, gq_ref[...], grad_query).astype(BF)
        gain_out[0:1, :] += jnp.sum(grad_query * raw * inverse_norm, axis=0, keepdims=True)
    grad_key = jnp.where(low, grad_keys[0], grad_keys[1])
    gain_out[1:2, :] += jnp.sum(grad_key * raw_key * inverse_key, axis=0, keepdims=True)
    gk_out[:, 0] = head_norm_back(raw_key, inverse_key, gk_ref[...], grad_key).astype(BF).reshape(shape)
    gv_out[:, 0] = jnp.where(low, grad_values[0], grad_values[1]).astype(BF).reshape(shape)


def attention_specs(rows, count):
    q_spec = pl.BlockSpec((1, rows, 2 * PAIR), lambda s, p: (s, 0, p))
    k_spec = pl.BlockSpec((count, 1, rows, PAIR), lambda s, p: (0, s, 0, p))
    v_spec = pl.BlockSpec((count, 1, rows, PAIR), lambda s, p: (0, s, 0, N_PAIRS + p))
    qs_spec = pl.BlockSpec((1, 1, rows), lambda s, p: (s, 0, 0))
    ks_spec = pl.BlockSpec((1, count, rows), lambda s, p: (s, 0, 0))
    gain_spec = pl.BlockSpec((1, PAIR), lambda s, p: (0, 0))
    return q_spec, k_spec, v_spec, qs_spec, ks_spec, gain_spec


def attention_cost(micro, rows, keys, products):
    work = micro * QUERY_HEADS * rows * keys
    return pl.CostEstimate(
        flops=2 * 4 * PAIR * products * work,
        bytes_accessed=micro * (rows * 6 * QUERY_COLUMNS + keys * 8 * KEY_COLUMNS),
        transcendentals=work,
    )


def attend(q, kv, q_seg, k_seg, gq, gk):
    count, micro, rows, _ = kv.shape
    q_spec, k_spec, v_spec, qs_spec, ks_spec, gain_spec = attention_specs(rows, count)
    return pl.pallas_call(
        forward_kernel,
        grid=(micro, N_PAIRS),
        in_specs=[q_spec, k_spec, v_spec, qs_spec, ks_spec, gain_spec, gain_spec],
        out_specs=q_spec,
        out_shape=jax.ShapeDtypeStruct((micro, rows, QUERY_COLUMNS), BF),
        cost_estimate=attention_cost(micro, rows, count * rows, 2),
        name="attend",
    )(q, kv, kv, q_seg, k_seg, gq, gk)


def attend_back(q, kv, grad_out, q_seg, k_seg, gq, gk):
    count, micro, rows, _ = kv.shape
    q_spec, k_spec, v_spec, qs_spec, ks_spec, gain_spec = attention_specs(rows, count)
    part = jax.ShapeDtypeStruct((count, micro, rows, KEY_COLUMNS), BF)
    return pl.pallas_call(
        backward_kernel,
        grid=(micro, N_PAIRS),
        in_specs=[q_spec, k_spec, v_spec, q_spec, qs_spec, ks_spec, gain_spec, gain_spec],
        out_specs=[q_spec, k_spec, k_spec, pl.BlockSpec((8, PAIR), lambda s, p: (0, 0))],
        out_shape=[
            jax.ShapeDtypeStruct((micro, rows, QUERY_COLUMNS), BF),
            part,
            part,
            jax.ShapeDtypeStruct((8, PAIR), F32),
        ],
        cost_estimate=attention_cost(micro, rows, count * rows, 5),
        name="attend_back",
    )(q, kv, kv, grad_out, q_seg, k_seg, gq, gk)


def far_blocks(block):
    size, me = lax.axis_size(FAR), lax.axis_index(FAR)
    if size > 4:
        return lax.all_gather(block, FAR, axis=0, tiled=False)
    found = [block]
    for distance in range(1, size):
        found.append(lax.ppermute(block, FAR, [(i, (i + distance) % size) for i in range(size)]))
    ordered = []
    for at in range(size):
        offset = (me - at) % size
        chosen = found[0]
        for distance in range(1, size):
            chosen = jnp.where(offset == distance, found[distance], chosen)
        ordered.append(chosen)
    return jnp.stack(ordered)


def far_parts(blocks):
    size, me = lax.axis_size(FAR), lax.axis_index(FAR)
    if size > 4:
        return [lax.psum_scatter(blocks, FAR, scatter_dimension=0, tiled=True)[0]]
    found = [pick(blocks, me, 0)]
    for distance in range(1, size):
        leaving = pick(blocks, (me + distance) % size, 0)
        found.append(lax.ppermute(leaving, FAR, [(i, (i + distance) % size) for i in range(size)]))
    return found


def exchange_sum(blocks, axis, index, at):
    other = swap(pick(blocks, 1 - index, at), axis)
    return (pick(blocks, index, at).astype(F32) + other.astype(F32)).astype(BF)


def lane_half(block, index):
    half = block.shape[-1] // 2
    return jnp.where(index == 0, block[..., :half], block[..., half:])


def exchange_lanes_sum(blocks, index):
    other = swap(lane_half(blocks, 1 - index), "wsh")
    return (lane_half(blocks, index).astype(F32) + other.astype(F32)).astype(BF)


def exchange(block, axis, index, at):
    return in_order(block, swap(block, axis), index, at)


def interleave_kernel(k_ref, mine_ref, other_ref, *outs):
    is_mine = pl.program_id(0) == k_ref[0]
    start = 0
    for out in outs:
        at = pl.ds(start, out.shape[2])
        start += out.shape[2]

        @pl.when(is_mine)
        def _(out=out, at=at):
            out[0, 0] = mine_ref[0, at, :]

        @pl.when(jnp.logical_not(is_mine))
        def _(out=out, at=at):
            out[0, 0] = other_ref[0, at, :]


def interleave(mine, other, k, widths):
    columns = mine.shape[-1]
    mine, other = (v.reshape(-1, sum(widths), columns) for v in (mine, other))
    count = mine.shape[0]

    def block_of(core):
        def index(c, i, k_ref):
            wanted = k_ref[0] if core == 0 else 1 - k_ref[0]
            return jnp.where(c == wanted, i, jnp.where(c < wanted, 0, count - 1)), 0, 0

        return pl.BlockSpec((1, sum(widths), columns), index)

    outs = pl.pallas_call(
        interleave_kernel,
        grid_spec=pltpu.PrefetchScalarGridSpec(
            num_scalar_prefetch=1,
            grid=(2, count),
            in_specs=[block_of(0), block_of(1)],
            out_specs=[pl.BlockSpec((1, 1, width, columns), lambda c, i, _: (i, c, 0, 0)) for width in widths],
        ),
        out_shape=[jax.ShapeDtypeStruct((count, 2, width, columns), BF) for width in widths],
        cost_estimate=pl.CostEstimate(flops=0, bytes_accessed=8 * mine.size, transcendentals=0),
        name="interleave",
    )(k.reshape(1).astype(jnp.int32), mine, other)
    return [v.reshape(-1, columns) for v in outs]


def gather_all(shards, index):
    n, k, w = index
    widths = [shard.shape[1] for shard in shards]
    part = far_blocks(jnp.concatenate([shard.astype(BF).T for shard in shards]))
    cut = part.shape[0] // 2
    one = exchange(part[:cut], "near", n, 1)
    two = exchange_lanes(part[cut:], w)
    one = exchange_lanes(one, w)
    two = exchange(two, "near", n, 1)
    firsts = interleave(one, swap(one, "core"), k, widths)
    seconds = interleave(two, swap(two, "core"), k, widths)
    return [half for pair in zip(firsts, seconds) for half in pair]


def grad_kernel(firsts, k_ref, *refs):
    groups = len(firsts) - 1
    keep, leave = refs[2 * groups :]
    width = keep.shape[1]
    for i in range(groups):

        @pl.when((pl.program_id(0) >= firsts[i]) & (pl.program_id(0) < firsts[i + 1]))
        def _(i=i):
            whole = dot_tn(refs[2 * i][...], refs[2 * i + 1][...])
            is_first = k_ref[0] == 0
            keep[0] = jnp.where(is_first, whole[:width], whole[width:]).astype(BF)
            leave[0] = jnp.where(is_first, whole[width:], whole[:width]).astype(BF)


def weight_grad(pairs, k):
    chips = lax.axis_size(FAR) * lax.axis_size("near")
    chip_width = sum(a.shape[1] for a, _ in pairs) // chips
    if chip_width % 128:
        whole = jnp.concatenate([dot_tn(a, b).astype(BF) for a, b in pairs])
        whole = whole.reshape(chips, 2, chip_width // 2, -1)
        return pick(whole, k, 1), pick(whole, 1 - k, 1)
    firsts, specs, operands = [0], [], []
    for a, b in pairs:
        start, count = firsts[-1], a.shape[1] // chip_width
        block = pl.BlockSpec(
            (a.shape[0], chip_width), lambda i, _, s=start, c=count: (0, jnp.clip(i - s, 0, c - 1))
        )
        specs += [block, pl.BlockSpec(b.shape, lambda i, _: (0, 0))]
        operands += [a, b]
        firsts.append(start + count)
    columns = pairs[0][1].shape[1]
    out = pl.BlockSpec((1, chip_width // 2, columns), lambda i, _: (i, 0, 0))
    shape = jax.ShapeDtypeStruct((chips, chip_width // 2, columns), BF)
    flops = sum(2 * a.shape[0] * a.shape[1] * columns for a, _ in pairs)
    return pl.pallas_call(
        functools.partial(grad_kernel, tuple(firsts)),
        grid_spec=pltpu.PrefetchScalarGridSpec(
            num_scalar_prefetch=1, grid=(chips,), in_specs=specs, out_specs=[out, out]
        ),
        out_shape=[shape, shape],
        cost_estimate=pl.CostEstimate(
            flops=flops, bytes_accessed=2 * sum(a.size + b.size for a, b in pairs) + 4 * chips * chip_width * columns, transcendentals=0
        ),
        name="weight_grad",
    )(k.reshape(1).astype(jnp.int32), *operands)


def scatter_all(grads, index):
    n, _, w = index
    keep, leave = grads
    far = lax.axis_size(FAR)
    cut = far // 2
    part = (keep.astype(F32) + swap(leave, "core").astype(F32)).astype(BF)
    part = part.reshape(far, 2, *part.shape[1:])
    one = exchange_sum(part[:cut], "near", n, 1)
    two = exchange_lanes_sum(part[cut:], w)
    one = exchange_lanes_sum(one, w)
    two = exchange_sum(two, "near", n, 1)
    return far_parts(jnp.concatenate([one, two]))


def exchange_lanes(block, index):
    other = swap(block, "wsh")
    first = jnp.concatenate([block, other], axis=-1)
    return jnp.where(index == 0, first, jnp.concatenate([other, block], axis=-1))


def gather_upgate(shard):
    whole = lax.all_gather(shard.astype(BF).T, OTHERS, axis=0, tiled=False)
    whole = whole.reshape(2, 2, -1, shard.shape[0])
    return [jnp.concatenate([whole[i, 0], whole[i, 1]], axis=1) for i in range(2)]


def scatter_upgate(grad_gate, grad_upper, tokens):
    half = D // 2
    halves = (tokens[:, :half], tokens[:, half:])
    blocks = jnp.stack([dot_tn(a, b).astype(BF) for a in (grad_gate, grad_upper) for b in halves])
    blocks = blocks.reshape(2 * lax.axis_size(OTHERS) // 2, -1, half)
    return [lax.psum_scatter(blocks, OTHERS, scatter_dimension=0, tiled=True)[0]]


CROSS = ((0, 0), (1, 2), (2, 1), (3, 3))


def cross(block):
    return lax.ppermute(block, ("top", "wsh"), CROSS)


def gather_down(shard, k):
    rows, width = shard.shape
    low = lax.axis_size("low")
    parts = cross(shard.astype(BF).T).reshape(width, 2 * low, 2, rows // (4 * low))
    both = in_order(pick(parts, k, 2), swap(pick(parts, 1 - k, 2), "core"), k)
    both = both.reshape(2 * width, rows // 2)
    return lax.all_gather(both, OTHERS, axis=0, tiled=True)


def scatter_down(grad, k):
    total = grad.shape[1]
    low = lax.axis_size("low")
    blocks = grad.reshape(lax.axis_size(OTHERS), -1, total)
    part = lax.psum_scatter(blocks, OTHERS, scatter_dimension=0, tiled=True)[0]
    width = part.shape[0] // 2
    parts = part.reshape(2, width, 2 * low, total // (2 * low))
    both = in_order(pick(parts, k, 0), swap(pick(parts, 1 - k, 0), "core"), k)
    return [cross(both.transpose(1, 2, 0, 3).reshape(width, 2 * total))]


def four_tokens(block):
    across = swap(block, "top")
    return jnp.concatenate([block, swap(block, "core"), across, swap(across, "core")])


def four_sum(partial):
    rows = partial.shape[0] // 4
    leaving = jnp.concatenate([partial[3 * rows :], partial[rows : 2 * rows]]).astype(BF)
    other = swap(leaving, "core").astype(F32)
    across = swap((partial[2 * rows : 3 * rows] + other[:rows]).astype(BF), "top")
    return partial[:rows] + other[rows:] + across.astype(F32)


def finish_kernel(early_ref, late_ref, m_ref, mean_ref, sq_ref, g_out, w_out, f_out, s_out, n_out, r_out):
    row = lax.broadcasted_iota(jnp.int32, (17, 128), 0)
    lane = lax.broadcasted_iota(jnp.int32, (17, 128), 1)
    grad = jnp.concatenate([late_ref[0:8, :], early_ref[0:8, :], late_ref[9:10, :]], axis=0)
    first, second, update = lamb_moments(grad, mean_ref[...], sq_ref[...])
    g_out[...] = grad
    f_out[...] = first
    s_out[...] = second
    master = m_ref[...]
    squares = early_ref[8:9, :] + late_ref[8:9, :]
    at = lax.broadcasted_iota(jnp.int32, (1, 128), 1)
    segment = jnp.where(row < 8, 0, jnp.where(row < 16, 1, jnp.where(lane < HEAD_WIDTH, 2, 3)))
    spot_row = lax.broadcasted_iota(jnp.int32, (2, 8), 0)
    spot_col = lax.broadcasted_iota(jnp.int32, (2, 8), 1)
    norms = jnp.zeros((2, 8), F32)
    ratio_lane = jnp.zeros((1, 128), F32)
    ratio_gain = jnp.zeros((17, 128), F32)
    for i in range(8):
        if i < 4:
            weight_sq = jnp.sum(jnp.where(at == i, squares, 0.0), keepdims=True)
            update_sq = jnp.sum(jnp.where(at == 4 + i, squares, 0.0), keepdims=True)
        else:
            weight_sq = jnp.sum(jnp.where(segment == i - 4, master * master, 0.0), keepdims=True)
            update_sq = jnp.sum(jnp.where(segment == i - 4, update * update, 0.0), keepdims=True)
        weight_norm, update_norm = jnp.sqrt(weight_sq), jnp.sqrt(update_sq)
        ratio = weight_norm / (update_norm + EPS_ADAM)
        norms = jnp.where(spot_col == i, jnp.where(spot_row == 0, weight_norm, update_norm), norms)
        if i < 4:
            ratio_lane = jnp.where(at == i, ratio, ratio_lane)
        else:
            ratio_gain = jnp.where(segment == i - 4, ratio, ratio_gain)
    n_out[...] = norms
    r_out[...] = ratio_lane
    w_out[...] = master - RATE * ratio_gain * update


def finish(early, late, master, mean, square):
    shaped = [v.reshape(17, 128) for v in (master, mean, square)]
    plane = jax.ShapeDtypeStruct((17, 128), F32)
    *gains, norms, ratios = pl.pallas_call(
        finish_kernel,
        out_shape=[plane] * 4 + [jax.ShapeDtypeStruct((2, 8), F32), jax.ShapeDtypeStruct((1, 128), F32)],
        name="finish",
    )(early, late, *shaped)
    return [g.reshape(GAINS) for g in gains], norms, ratios[0]


def moments_kernel(which, steps, count, turn, *refs):
    parts = refs[:count]
    m_ref, s_ref, w_ref, g_out, f_out, s_out, u_out, sum_out, acc = refs[count:]
    step = pl.program_id(0)

    @pl.when(step == 0)
    def _():
        acc[...] = jnp.zeros_like(acc)

    grad = parts[0][...].astype(F32)
    for part in parts[1:]:
        grad += part[...].astype(F32)
    if turn:
        grad = grad.T
    master = w_ref[...]
    first, second, direction = lamb_moments(grad, m_ref[...], s_ref[...])
    update = direction + DECAY * master
    g_out[...] = grad
    f_out[...] = first
    s_out[...] = second
    u_out[...] = update
    acc[0:1, :] += jnp.sum(master * master, axis=0, keepdims=True)
    acc[1:2, :] += jnp.sum(update * update, axis=0, keepdims=True)

    @pl.when(step == steps - 1)
    def _():
        lane = lax.broadcasted_iota(jnp.int32, (1, 128), 1)
        master_sum = jnp.sum(acc[0:1, :], keepdims=True)
        update_sum = jnp.sum(acc[1:2, :], keepdims=True)
        sum_out[...] = jnp.where(lane == which, master_sum, jnp.where(lane == 4 + which, update_sum, 0.0))


def moments(which, parts, mean, square, master):
    rows, columns = master.shape
    turn = columns % 128 == 0
    steps = 4 if rows % 512 == 0 else 6
    if rows % (128 * steps):
        steps = 1
    tall = pl.BlockSpec((columns, rows // steps), lambda i: (0, i))
    block = pl.BlockSpec((rows // steps, columns), lambda i: (i, 0)) if turn else tall
    others = (mean, square, master) if turn else (mean.T, square.T, master.T)
    plane = jax.ShapeDtypeStruct(others[0].shape, F32)
    *outs, sums = pl.pallas_call(
        functools.partial(moments_kernel, which, steps, len(parts), turn),
        grid=(steps,),
        in_specs=[tall] * len(parts) + [block] * 3,
        out_specs=[block] * 4 + [pl.BlockSpec((1, 128), lambda i: (0, 0))],
        out_shape=[plane] * 4 + [jax.ShapeDtypeStruct((1, 128), F32)],
        scratch_shapes=[pltpu.VMEM((2, block.block_shape[1]), F32)],
        cost_estimate=pl.CostEstimate(
            flops=20 * rows * columns, bytes_accessed=32 * rows * columns, transcendentals=2 * rows * columns
        ),
        name="moments",
    )(*parts, *others)
    return *(outs if turn else [o.T for o in outs]), sums


def local(
    tokens, segment_ids, cotangent,
    qkv_master, qkv_mean, qkv_square,
    proj_master, proj_mean, proj_square,
    upgate_master, upgate_mean, upgate_square,
    down_master, down_mean, down_square,
    gain_master, gain_mean, gain_square,
):
    micro, extent, _ = tokens.shape
    rows = micro * extent
    n_ctx = lax.axis_size(CTX)
    depth = n_ctx // 4
    n, k, w = (lax.axis_index(a) for a in ("near", "core", "wsh"))
    index = (n, k, w)
    half = D // 2
    attn_gain = gain_master[:D]
    ffn_gain = gain_master[D : 2 * D]
    query_gain = gain_master[2 * D : 2 * D + HEAD_WIDTH]
    key_gain = gain_master[2 * D + HEAD_WIDTH :]
    gq = jnp.tile(query_gain, 2)[None]
    gk = jnp.tile(key_gain, 2)[None]

    extra = jnp.pad(segment_ids.astype(BF).reshape(1, rows), ((0, 15), (0, D - rows)))
    package = jnp.concatenate([tokens.reshape(rows, D), extra])
    halo, exists = from_earlier(package, depth)
    query_t, kv_t, *proj_t = gather_all((qkv_master, proj_master), index)
    gate_t, up_t = gather_upgate(upgate_master)
    down_t = gather_down(down_master, k)

    count = depth + 1
    around = jnp.concatenate([came[:rows] for came in halo] + [package[:rows]]).astype(F32)
    seg_rows = jnp.concatenate([came[rows : rows + 1, :rows] for came in halo] + [package[rows : rows + 1, :rows]])
    row = lax.broadcasted_iota(jnp.int32, (count, rows), 0)
    present = row == depth
    for i, there in enumerate(exists):
        present = present | ((row == i) & there)
    k_seg = jnp.where(present, seg_rows.astype(F32), -1.0).reshape(count, micro, extent).transpose(1, 0, 2)
    q_seg = segment_ids[:, None, :].astype(F32)
    normed_around = lax.optimization_barrier(rms_norm(around, attn_gain)[0].astype(BF))
    inputs = tokens.astype(F32).reshape(rows, D)
    inv_one = lax.rsqrt(jnp.mean(inputs * inputs, axis=-1, keepdims=True) + EPS_NORM)
    normed_low = normed_around[depth * rows :]
    q_raw = dot_nt(normed_low, query_t).reshape(micro, extent, QUERY_COLUMNS)
    kv_raw = dot_nt(normed_around, kv_t).reshape(count, micro, extent, 2 * KEY_COLUMNS)
    attn_low = attend(q_raw, kv_raw, q_seg, k_seg, gq, gk).reshape(rows, QUERY_COLUMNS)

    cot_low = cotangent.reshape(rows, D)
    cot_four = four_tokens(cot_low)
    middle = inputs + jnp.concatenate([dot_nt(attn_low, p) for p in proj_t], axis=1)
    normed_two, inv_two = rms_norm(middle, ffn_gain)
    two_four = four_tokens(normed_two.astype(BF))
    gate = dot_nt(two_four, gate_t)
    upper = dot_nt(two_four, up_t)
    grad_hidden = dot_nn(cot_four, down_t)
    sigmoid_gate = jax.nn.sigmoid(gate)
    activated = gate * sigmoid_gate
    hidden_low = (activated * upper).astype(BF)
    grad_gate = (grad_hidden * upper * sigmoid_gate * (1.0 + gate * (1.0 - sigmoid_gate))).astype(BF)
    grad_upper = (grad_hidden * activated).astype(BF)
    grad_two_part = dot_nn(grad_gate, gate_t) + dot_nn(grad_upper, up_t)
    grad_two = four_sum(grad_two_part)
    upgate_parts = scatter_upgate(grad_gate, grad_upper, two_four)
    down_parts = scatter_down(dot_tn(cot_four, hidden_low).astype(BF), k)
    block_out = (lax.optimization_barrier(middle) + four_sum(dot_nt(hidden_low, down_t))).astype(BF).reshape(tokens.shape)

    grad_middle, ffn_rows = norm_back(middle, inv_two, ffn_gain, grad_two)
    grad_middle = grad_middle + cot_low.astype(F32)
    grad_middle_low = grad_middle.astype(BF)
    proj_parts = scatter_all(weight_grad([(grad_middle_low, attn_low)], k), index)
    grad_attn = dot_nn(grad_middle_low[:, :half], proj_t[0]) + dot_nn(grad_middle_low[:, half:], proj_t[1])
    grad_attn = grad_attn.astype(BF).reshape(micro, extent, QUERY_COLUMNS)
    grad_q, gk_part, gv_part, head_rows = attend_back(q_raw, kv_raw, grad_attn, q_seg, k_seg, gq, gk)
    grad_q = grad_q.reshape(rows, QUERY_COLUMNS)
    gk_all = gk_part.reshape(count * rows, KEY_COLUMNS)
    gv_all = gv_part.reshape(count * rows, KEY_COLUMNS)
    pieces = [(grad_q, normed_low), (gk_all, normed_around), (gv_all, normed_around)]
    qkv_parts = scatter_all(weight_grad(pieces, k), index)
    grad_kv = jnp.concatenate([gk_all, gv_all], axis=1).reshape(count, rows, 2 * KEY_COLUMNS)
    total_kv = to_earlier([grad_kv[i] for i in range(depth)], grad_kv[depth].astype(F32))
    total_kv = total_kv.astype(BF)
    grad_normed = dot_nn(grad_q, query_t) + dot_nn(total_kv, kv_t)
    grad_in, attn_rows = norm_back(inputs, inv_one, attn_gain, grad_normed)
    input_grad = (grad_middle + grad_in).reshape(tokens.shape)

    masters = (qkv_master, proj_master, upgate_master, down_master)
    parts = (qkv_parts, proj_parts, upgate_parts, down_parts)
    means = (qkv_mean, proj_mean, upgate_mean, down_mean)
    squares = (qkv_square, proj_square, upgate_square, down_square)
    moved = [moments(i, parts[i], means[i], squares[i], masters[i]) for i in range(4)]
    heads_row = head_rows[0:2, :HEAD_WIDTH] + head_rows[0:2, HEAD_WIDTH:]
    early_row = moved[1][4] + moved[2][4] + moved[3][4]
    early = jnp.concatenate([jnp.sum(ffn_rows, axis=0).reshape(8, 128), early_row])
    late = jnp.concatenate([jnp.sum(attn_rows, axis=0).reshape(8, 128), moved[0][4], heads_row.reshape(1, 128)])
    early, late = total_everywhere(early), total_everywhere(late)
    early_norms = jnp.sqrt(early[8])
    gain_outs, lamb_norms, ratios = finish(early, late, gain_master, gain_mean, gain_square)
    gain_grad, gain_weight, gain_first, gain_second = gain_outs
    outs = [block_out, input_grad]
    for i in range(4):
        ratio = ratios[0] if i == 0 else early_norms[i] / (early_norms[4 + i] + EPS_ADAM)
        grad, first, second, update, _ = moved[i]
        outs += [grad, masters[i] - RATE * ratio * update, first, second]
    return (*outs, gain_grad, gain_weight, gain_first, gain_second, lamb_norms)


def solution(mesh):
    n_ctx, n_wsh = mesh.devices.shape
    fine = Mesh(mesh.devices.reshape(2, 2, n_ctx // 16, 2, 2, n_wsh), EVERY)
    sequence = P("wsh", CTX)
    weight = P("wsh", CTX)
    return jax.shard_map(
        local,
        mesh=fine,
        in_specs=(sequence,) * 3 + (weight,) * 12 + (P(),) * 3,
        out_specs=(sequence,) * 2 + (weight,) * 16 + (P(),) * 5,
        check_vma=False,
    )
```

profile of v0, /device:TPU:0, one launch (start us, length us, event | category | flops | bytes accessed | tf_op | source)
XLA Modules:
  0.0 483.4 jit_solution(7441530174888682412)
XLA Ops:
  9.8 5.1 %collective-permute-start.4 = (bf16[192,512]{1,0:T(8,128)(2,1)S(1)}, bf16[192,512]{1,0:T(8,128)(2,1)S(1)}, u32[]{:S(2)}, u32[]{:S(2)}) collective-permute-start(bf16[192,512]{1,0:T(8,128)(2,1)S(1)} %pad_maximum_fusion.16), channel_id=1, source_target_pairs={{0,24},{8,0},{16,8},{24,16},{1,25},{9,1},{17,9},{25,17},{2,26},{10... | collective-permute-start | bytes 589832 | tf_op jit(solution)/shard_map/ppermute | solution.py:305
  17.4 4.4 collective-permute-start
  23.9 16.0 %collective-permute-done.5 = bf16[192,512]{1,0:T(8,128)(2,1)S(1)} collective-permute-done((bf16[192,512]{1,0:T(8,128)(2,1)S(1)}, bf16[192,512]{1,0:T(8,128)(2,1)S(1)}, u32[]{:S(2)}, u32[]{:S(2)}) %collective-permute-start.5) | collective-permute-done | bytes 196640 | tf_op jit(solution)/shard_map/ppermute | solution.py:305
  44.5 18.5 %collective-permute-start.10 = (bf16[2,192,512]{2,1,0:T(8,128)(2,1)}, bf16[2,192,512]{2,1,0:T(8,128)(2,1)S(1)}, u32[]{:S(2)}, u32[]{:S(2)}) collective-permute-start(bf16[2,192,512]{2,1,0:T(8,128)(2,1)} %get-tuple-element.141), channel_id=1, source_target_pairs={{0,1},{1,0},{2,3},{3,2},{4,5},{5,4},{6,7},{7,6},{8,9},{9,8},{10,11... | collective-permute-start | bytes 1179656 | tf_op jit(solution)/shard_map/ppermute | solution.py:42
  66.6 7.6 %collective-permute-start.8 = (bf16[2,2,192,512]{3,2,1,0:T(8,128)(2,1)S(1)}, bf16[2,2,192,512]{3,2,1,0:T(8,128)(2,1)S(1)}, u32[]{:S(2)}, u32[]{:S(2)}) collective-permute-start(bf16[2,2,192,512]{3,2,1,0:T(8,128)(2,1)S(1)} %maximum_select_fusion.3), channel_id=1, source_target_pairs={{0,1},{1,0},{2,3},{3,2},{4,5},{5,4},{6,7},{7,6},{8,9},{9,8},{10,11... | collective-permute-start | bytes 2359304 | tf_op jit(solution)/shard_map/ppermute | solution.py:42
  76.3 6.5 %collective-permute-done.1 = bf16[272,1024]{1,0:T(8,128)(2,1)S(1)} collective-permute-done((bf16[272,1024]{1,0:T(8,128)(2,1)S(1)}, bf16[272,1024]{1,0:T(8,128)(2,1)S(1)}, u32[]{:S(2)}, u32[]{:S(2)}) %collective-permute-start.1) | collective-permute-done | bytes 557088 | tf_op jit(solution)/shard_map/ppermute | solution.py:42
  82.9 23.9 %collective-permute-done.8 = bf16[2,2,192,512]{3,2,1,0:T(8,128)(2,1)S(1)} collective-permute-done((bf16[2,2,192,512]{3,2,1,0:T(8,128)(2,1)S(1)}, bf16[2,2,192,512]{3,2,1,0:T(8,128)(2,1)S(1)}, u32[]{:S(2)}, u32[]{:S(2)}) %collective-permute-start.8) | collective-permute-done | bytes 786464 | tf_op jit(solution)/shard_map/ppermute | solution.py:42
  108.5 4.5 collective-permute-done.11
  118.9 6.5 %interleave.2 = (bf16[4,2,128,1024]{3,2,1,0:T(8,128)(2,1)}, bf16[4,2,64,1024]{3,2,1,0:T(8,128)(2,1)}) custom-call(s32[1]{0:T(128)} %bitcast.3.k_ref, bf16[4,192,1024]{2,1,0:T(8,128)(2,1)} %maximum_select_fusion.mine_ref, bf16[4,192,1024]{2,1,0:T(8,128)(2,1)} %bitcast.12.other_ref), custom_call_target="tpu_custom_call" | custom-call | bytes 6291456 | tf_op jit(solution)/shard_map/interleave/pallas_call | solution.py:374
  125.4 3.3 fusion.100.q_ref
  128.7 6.5 %interleave.3 = (bf16[4,2,128,1024]{3,2,1,0:T(8,128)(2,1)}, bf16[4,2,64,1024]{3,2,1,0:T(8,128)(2,1)}) custom-call(s32[1]{0:T(128)} %bitcast.3.k_ref, bf16[4,192,1024]{2,1,0:T(8,128)(2,1)} %bitcast.256, bf16[4,192,1024]{2,1,0:T(8,128)(2,1)} %bitcast.22.other_ref), custom_call_target="tpu_custom_call" | custom-call | bytes 6291456 | tf_op jit(solution)/shard_map/interleave/pallas_call | solution.py:374
  135.3 6.3 %fusion.101.k_ref.v_ref = f32[5,2,128,1024]{3,2,1,0:T(8,128)} fusion(bf16[5,2,128,1024]{3,2,1,0:T(8,128)(2,1)S(1)} %bitcast.268, bf16[1024,1024,1,1]{1,0,3,2:T(8,128)(2,1)} %bitcast.278), kind=kOutput, calls=%fused_computation.244 | convolution fusion | flops 2684354560 | bytes 9961472 | tf_op jit(solution)/shard_map/dot_general | solution.py:124
  141.6 14.4 %attend.1 = bf16[2,128,1024]{2,1,0:T(8,128)(2,1)} custom-call(f32[2,128,1024]{2,1,0:T(8,128)} %fusion.100.q_ref, f32[5,2,128,1024]{3,2,1,0:T(8,128)} %fusion.101.k_ref.v_ref, f32[5,2,128,1024]{3,2,1,0:T(8,128)} %fusion.101.k_ref.v_ref, f32[2,1,128]{2,1,0:T(1,128)} %bitcast.312, f32[2,5,128]{2,1,0:T(8,128)} %select_bitcast_fusion.4.ks_ref, ...), custom_call_target="tpu_custom_call" | custom-call | flops 5368709120 | bytes 6815744 | tf_op jit(solution)/shard_map/attend/pallas_call | solution.py:268
  158.6 7.0 %collective-permute-start.14 = (bf16[256,1024]{1,0:T(8,128)(2,1)S(1)}, bf16[256,1024]{1,0:T(8,128)(2,1)}, u32[]{:S(2)}, u32[]{:S(2)}) collective-permute-start(bf16[256,1024]{1,0:T(8,128)(2,1)S(1)} %get-tuple-element.108), channel_id=1, source_target_pairs={{0,8},{8,0},{1,9},{9,1},{2,10},{10,2},{3,11},{11,3},{4,12},{12,4},... | collective-permute-start | bytes 1572872 | tf_op jit(solution)/shard_map/ppermute | solution.py:42
  165.9 16.4 %collective-permute-done.14 = bf16[256,1024]{1,0:T(8,128)(2,1)} collective-permute-done((bf16[256,1024]{1,0:T(8,128)(2,1)S(1)}, bf16[256,1024]{1,0:T(8,128)(2,1)}, u32[]{:S(2)}, u32[]{:S(2)}) %collective-permute-start.14) | collective-permute-done | bytes 524320 | tf_op jit(solution)/shard_map/ppermute | solution.py:42
  182.9 10.7 %collective-permute-done.21 = bf16[256,1024]{1,0:T(8,128)(2,1)} collective-permute-done((bf16[256,1024]{1,0:T(8,128)(2,1)}, bf16[256,1024]{1,0:T(8,128)(2,1)}, u32[]{:S(2)}, u32[]{:S(2)}) %collective-permute-start.21) | collective-permute-done | bytes 524320 | tf_op jit(solution)/shard_map/ppermute | solution.py:42
  193.7 2.8 pad_maximum_fusion.3
  196.6 2.6 slice_bitcast_fusion.3
  199.3 7.6 %fusion.10 = f32[1024,1152]{1,0:T(8,128)} fusion(bf16[1152,512]{1,0:T(8,128)(2,1)S(1)} %get-tuple-element.116, bf16[1152,512]{1,0:T(8,128)(2,1)S(1)} %get-tuple-element.113, bf16[256,1024]{1,0:T(8,128)(2,1)} %collective-permute-done.15, bf16[256,1024]{1,0:T(8,128)(2,1)} %collective-permute-done.14, bf16[256,1024]{1,0:T(8,128)(2,1)} %collective-permute-done.13, ...), kind=kOutput, calls=%fused_computation.40 | convolution fusion | flops 2429026304 | bytes 9175040 | tf_op jit(solution)/shard_map/dot_general | solution.py:124
  206.9 6.4 %fusion.8 = f32[1024,1152]{1,0:T(8,128)} fusion(bf16[1152,512]{1,0:T(8,128)(2,1)S(1)} %get-tuple-element.114, bf16[1152,512]{1,0:T(8,128)(2,1)S(1)} %get-tuple-element.115, bf16[256,1024]{1,0:T(8,128)(2,1)} %collective-permute-done.15, bf16[256,1024]{1,0:T(8,128)(2,1)} %collective-permute-done.14, bf16[256,1024]{1,0:T(8,128)(2,1)} %collective-permute-done.13, ...), kind=kOutput, calls=%fused_computation.38 | convolution fusion | flops 2429026304 | bytes 9175040 | tf_op jit(solution)/shard_map/dot_general | solution.py:124
  213.3 10.4 %multiply_convert_fusion = (bf16[1024,1152]{1,0:T(8,128)(2,1)}, bf16[1024,1152]{1,0:T(8,128)(2,1)}, bf16[1024,1152]{1,0:T(8,128)(2,1)S(1)}) fusion(f32[1024,1152]{1,0:T(8,128)} %fusion.10, f32[1024,1152]{1,0:T(8,128)} %fusion.8, bf16[1024,1152]{1,0:T(8,128)(2,1)} %all-gather.4.cloned.1.call-done, bf16[256,1024]{1,0:T(8,128)(2,1)} %collective-permute-done.22, ...), kind=kOutput, calls=%fused_computation.6 | convolution fusion | flops 2442002432 | bytes 20971520 | tf_op jit(solution)/shard_map/dot_general | solution.py:132
  223.7 6.7 %convolution_convert_fusion = bf16[1024,1152]{1,0:T(8,128)(2,1)} fusion(bf16[1024,1152]{1,0:T(8,128)(2,1)S(1)} %get-tuple-element.112, bf16[256,1024]{1,0:T(8,128)(2,1)} %collective-permute-done.22, bf16[256,1024]{1,0:T(8,128)(2,1)} %collective-permute-done.21, bf16[256,1024]{1,0:T(8,128)(2,1)} %collective-permute-done.20, bf16[256,1024]{1,0:T(8,128)(2,1)} %bitcast.50), kind=kOutput, calls=%fused_computation.12 | convolution fusion | flops 2425487360 | bytes 6815744 | tf_op jit(solution)/shard_map/dot_general | solution.py:128
  230.5 7.5 %fusion.98 = (bf16[1024,1024]{1,0:T(8,128)(2,1)S(1)}, f32[1024,1024]{1,0:T(8,128)}) fusion(bf16[1024,1152]{1,0:T(8,128)(2,1)} %copy-done.61, bf16[1024,1152]{1,0:T(8,128)(2,1)} %all-gather.4.cloned.1.call-done), kind=kOutput, calls=%fused_computation.241 | convolution fusion | flops 2416967680 | bytes 11010048 | tf_op jit(solution)/shard_map/dot_general | solution.py:124
  240.0 2.9 fusion.9
  242.9 2.9 fusion.99
  246.4 2.5 copy-done.23
  257.1 2.9 pad_maximum_fusion
  267.2 9.2 %collective-permute-done.24 = bf16[256,1024]{1,0:T(8,128)(2,1)S(1)} collective-permute-done((bf16[256,1024]{1,0:T(8,128)(2,1)}, bf16[256,1024]{1,0:T(8,128)(2,1)S(1)}, u32[]{:S(2)}, u32[]{:S(2)}) %collective-permute-start.24) | collective-permute-done | bytes 524320 | tf_op jit(solution)/shard_map/ppermute | solution.py:42
  278.0 2.5 fusion.87
  280.6 6.4 %weight_grad.3 = (bf16[8,64,1024]{2,1,0:T(8,128)(2,1)}, bf16[8,64,1024]{2,1,0:T(8,128)(2,1)}) custom-call(s32[1]{0:T(128)} %bitcast.3.k_ref, bf16[256,1024]{1,0:T(8,128)(2,1)} %get-tuple-element.105.refs_0_, bf16[256,1024]{1,0:T(8,128)(2,1)} %bitcast.281), custom_call_target="tpu_custom_call" | custom-call | flops 536870912 | bytes 5242880 | tf_op jit(solution)/shard_map/weight_grad/pallas_call | solution.py:437
  289.6 24.8 %attend_back.1 = (bf16[2,128,1024]{2,1,0:T(8,128)(2,1)}, bf16[5,2,128,512]{3,2,1,0:T(8,128)(2,1)}, bf16[5,2,128,512]{3,2,1,0:T(8,128)(2,1)}, f32[8,128]{1,0:T(8,128)}) custom-call(f32[2,128,1024]{2,1,0:T(8,128)} %fusion.100.q_ref, f32[5,2,128,1024]{3,2,1,0:T(8,128)} %fusion.101.k_ref.v_ref, f32[5,2,128,1024]{3,2,1,0:T(8,128)} %fusion.101.k_ref.v_ref, ...), custom_call_target="tpu_custom_call" | custom-call | flops 13421772800 | bytes 6815744 | tf_op jit(solution)/shard_map/attend_back/pallas_call | solution.py:283
  317.2 11.1 %weight_grad.2 = (bf16[8,128,1024]{2,1,0:T(8,128)(2,1)}, bf16[8,128,1024]{2,1,0:T(8,128)(2,1)}) custom-call(s32[1]{0:T(128)} %bitcast.3.k_ref, bf16[256,1024]{1,0:T(8,128)(2,1)} %bitcast.293, bf16[256,1024]{1,0:T(8,128)(2,1)} %copy-done.22, bf16[1280,512]{1,0:T(8,128)(2,1)} %bitcast.242, bf16[1280,1024]{1,0:T(8,128)(2,1)} %copy-done.18, ...), custom_call_target="tpu_custom_call" | custom-call | flops 3221225472 | bytes 17301504 | tf_op jit(solution)/shard_map/weight_grad/pallas_call | solution.py:437
  335.9 4.4 collective-permute-done.40
  341.8 20.3 %collective-permute-done.38 = bf16[2,64,1024]{2,1,0:T(8,128)(2,1)S(1)} collective-permute-done((bf16[2,64,1024]{2,1,0:T(8,128)(2,1)S(1)}, bf16[2,64,1024]{2,1,0:T(8,128)(2,1)S(1)}, u32[]{:S(2)}, u32[]{:S(2)}) %collective-permute-start.38) | collective-permute-done | bytes 262176 | tf_op jit(solution)/shard_map/ppermute | solution.py:42
  363.8 3.3 collective-permute-done.41
  368.7 5.9 %collective-permute-done.39 = bf16[2,64,512]{2,1,0:T(8,128)(2,1)S(1)} collective-permute-done((bf16[2,64,512]{2,1,0:T(8,128)(2,1)S(1)}, bf16[2,64,512]{2,1,0:T(8,128)(2,1)S(1)}, u32[]{:S(2)}, u32[]{:S(2)}) %collective-permute-start.39) | collective-permute-done | bytes 131104 | tf_op jit(solution)/shard_map/ppermute | solution.py:42
  383.8 3.4 moments.5
  387.3 3.2 add_convert_fusion
  394.3 3.0 fusion.41
  397.3 3.8 collective-permute-done.30
  401.4 2.5 collective-permute-start.31
  413.6 3.2 collective-permute-start.34
  421.2 3.8 fusion.35
  427.2 3.8 moments.4
  432.4 5.4 %moments.7 = (f32[64,2304]{1,0:T(8,128)}, f32[64,2304]{1,0:T(8,128)}, f32[64,2304]{1,0:T(8,128)}, f32[64,2304]{1,0:T(8,128)}, f32[1,128]{1,0:T(1,128)}) custom-call(bf16[64,2304]{1,0:T(8,128)(2,1)} %copy-done.43, f32[64,2304]{1,0:T(8,128)} %bitcast.290, f32[64,2304]{1,0:T(8,128)} %bitcast.291, f32[64,2304]{1,0:T(8,128)} %bitcast.257), custom_call_target="tpu_custom_call" | custom-call | flops 2949120 | bytes 4718592 | tf_op jit(solution)/shard_map/moments/pallas_call | solution.py:613
  437.9 5.6 %moments.6 = (f32[576,512]{1,0:T(8,128)}, f32[576,512]{1,0:T(8,128)}, f32[576,512]{1,0:T(8,128)}, f32[576,512]{1,0:T(8,128)}, f32[1,128]{1,0:T(1,128)}) custom-call(bf16[576,512]{1,0:T(8,128)(2,1)} %bitcast.292, f32[576,512]{1,0:T(8,128)} %bitcast.285, f32[576,512]{1,0:T(8,128)} %bitcast.286, f32[576,512]{1,0:T(8,128)} %bitcast.252), custom_call_target="tpu_custom_call" | custom-call | flops 5898240 | bytes 9437184 | tf_op jit(solution)/shard_map/moments/pallas_call | solution.py:613
  444.9 2.7 collective-permute-start.53
  452.4 2.8 fusion.25
  (359 shorter events, 119.6 us)
Async XLA Ops:
  7.3 189.3 %all-gather.6.cloned.1.call-start = ((), (), s32[]{:S(2)}) async-start(), calls=%async_computation.5 | async-start | bytes 5308416 | tf_op jit(solution)/shard_map/all_gather | solution.py:471
  9.6 203.7 %all-gather.4.cloned.1.call-start = ((), (), s32[]{:S(2)}) async-start(), calls=%async_computation.2 | async-start | bytes 2654208 | tf_op jit(solution)/shard_map/all_gather | solution.py:497
  9.8 14.1 %collective-permute-start.4 = (bf16[192,512]{1,0:T(8,128)(2,1)S(1)}, bf16[192,512]{1,0:T(8,128)(2,1)S(1)}, u32[]{:S(2)}, u32[]{:S(2)}) collective-permute-start(bf16[192,512]{1,0:T(8,128)(2,1)S(1)} %pad_maximum_fusion.16), channel_id=1, source_target_pairs={{0,24},{8,0},{16,8},{24,16},{1,25},{9,1},{17,9},{25,17},{2,26},{10... | collective-permute-start | bytes 589832 | tf_op jit(solution)/shard_map/ppermute | solution.py:305
  14.9 25.0 %collective-permute-start.5 = (bf16[192,512]{1,0:T(8,128)(2,1)S(1)}, bf16[192,512]{1,0:T(8,128)(2,1)S(1)}, u32[]{:S(2)}, u32[]{:S(2)}) collective-permute-start(bf16[192,512]{1,0:T(8,128)(2,1)S(1)} %pad_maximum_fusion.16), channel_id=1, source_target_pairs={{0,16},{8,24},{16,0},{24,8},{1,17},{9,25},{17,1},{25,9},{2,18},{10... | collective-permute-start | bytes 589832 | tf_op jit(solution)/shard_map/ppermute | solution.py:305
  14.9 25.0 %collective-permute-start.6 = (bf16[192,512]{1,0:T(8,128)(2,1)S(1)}, bf16[192,512]{1,0:T(8,128)(2,1)S(1)}, u32[]{:S(2)}, u32[]{:S(2)}) collective-permute-start(bf16[192,512]{1,0:T(8,128)(2,1)S(1)} %pad_maximum_fusion.16), channel_id=1, source_target_pairs={{0,8},{8,16},{16,24},{24,0},{1,9},{9,17},{17,25},{25,1},{2,10},{10... | collective-permute-start | bytes 589832 | tf_op jit(solution)/shard_map/ppermute | solution.py:305
  17.4 47.2 %collective-permute-start = (bf16[272,1024]{1,0:T(8,128)(2,1)}, bf16[272,1024]{1,0:T(8,128)(2,1)S(1)}, u32[]{:S(2)}, u32[]{:S(2)}) collective-permute-start(bf16[272,1024]{1,0:T(8,128)(2,1)} %fusion.40), channel_id=1, source_target_pairs={{0,8},{8,16},{16,24},{1,9},{9,17},{17,25},{2,10},{10,18},{18,26},{... | collective-permute-start | bytes 1671176 | tf_op jit(solution)/shard_map/ppermute | solution.py:55
  21.8 18.4 %collective-permute-start.16 = (bf16[64,2304]{1,0:T(8,128)(2,1)S(1)}, bf16[64,2304]{1,0:T(8,128)(2,1)S(1)}, u32[]{:S(2)}, u32[]{:S(2)}) collective-permute-start(bf16[64,2304]{1,0:T(8,128)(2,1)S(1)} %convert_bitcast_fusion.1), channel_id=1, source_target_pairs={{0,0},{1,8},{8,1},{9,9},{2,2},{3,10},{10,3},{11,11},{4,4},{5,12},{... | collective-permute-start | bytes 884744 | tf_op jit(solution)/shard_map/ppermute | solution.py:488
  41.3 21.7 %collective-permute-start.17 = (bf16[64,2,576]{2,0,1:T(8,128)(2,1)S(1)}, bf16[64,2,576]{2,0,1:T(8,128)(2,1)S(1)}, u32[]{:S(2)}, u32[]{:S(2)}) collective-permute-start(bf16[64,2,576]{2,0,1:T(8,128)(2,1)S(1)} %bitcast.299), channel_id=1, source_target_pairs={{0,2},{2,0},{1,3},{3,1},{4,6},{6,4},{5,7},{7,5},{8,10},{10,8},{9,1... | collective-permute-start | bytes 442376 | tf_op jit(solution)/shard_map/ppermute | solution.py:42
  42.2 23.2 %collective-permute-start.7 = (bf16[2,192,512]{2,1,0:T(8,128)(2,1)}, bf16[2,192,512]{2,1,0:T(8,128)(2,1)}, u32[]{:S(2)}, u32[]{:S(2)}) collective-permute-start(bf16[2,192,512]{2,1,0:T(8,128)(2,1)} %get-tuple-element.143), channel_id=1, source_target_pairs={{0,4},{4,0},{1,5},{5,1},{2,6},{6,2},{3,7},{7,3},{8,12},{12,8},{9,1... | collective-permute-start | bytes 1179656 | tf_op jit(solution)/shard_map/ppermute | solution.py:42
  44.5 29.8 %collective-permute-start.10 = (bf16[2,192,512]{2,1,0:T(8,128)(2,1)}, bf16[2,192,512]{2,1,0:T(8,128)(2,1)S(1)}, u32[]{:S(2)}, u32[]{:S(2)}) collective-permute-start(bf16[2,192,512]{2,1,0:T(8,128)(2,1)} %get-tuple-element.141), channel_id=1, source_target_pairs={{0,1},{1,0},{2,3},{3,2},{4,5},{5,4},{6,7},{7,6},{8,9},{9,8},{10,11... | collective-permute-start | bytes 1179656 | tf_op jit(solution)/shard_map/ppermute | solution.py:42
  64.5 343.9 %reduce-scatter.5.cloned.1.call-start = ((), (), s32[]{:S(2)}) async-start(), calls=%async_computation.4 | async-start | bytes 2654208 | tf_op jit(solution)/shard_map/reduce_scatter | solution.py:504
  64.8 18.0 %collective-permute-start.1 = (bf16[272,1024]{1,0:T(8,128)(2,1)S(1)}, bf16[272,1024]{1,0:T(8,128)(2,1)S(1)}, u32[]{:S(2)}, u32[]{:S(2)}) collective-permute-start(bf16[272,1024]{1,0:T(8,128)(2,1)S(1)} %get-tuple-element.126), channel_id=1, source_target_pairs={{0,4},{4,0},{1,5},{5,1},{2,6},{6,2},{3,7},{7,3},{8,12},{12,8},{9,1... | collective-permute-start | bytes 1671176 | tf_op jit(solution)/shard_map/ppermute | solution.py:42
  65.3 17.5 %collective-permute-start.2 = (bf16[272,1024]{1,0:T(8,128)(2,1)S(1)}, bf16[272,1024]{1,0:T(8,128)(2,1)S(1)}, u32[]{:S(2)}, u32[]{:S(2)}) collective-permute-start(bf16[272,1024]{1,0:T(8,128)(2,1)S(1)} %get-tuple-element.125), channel_id=1, source_target_pairs={{0,2},{2,0},{1,3},{3,1},{4,6},{6,4},{5,7},{7,5},{8,10},{10,8},{9,1... | collective-permute-start | bytes 1671176 | tf_op jit(solution)/shard_map/ppermute | solution.py:42
  66.6 40.2 %collective-permute-start.8 = (bf16[2,2,192,512]{3,2,1,0:T(8,128)(2,1)S(1)}, bf16[2,2,192,512]{3,2,1,0:T(8,128)(2,1)S(1)}, u32[]{:S(2)}, u32[]{:S(2)}) collective-permute-start(bf16[2,2,192,512]{3,2,1,0:T(8,128)(2,1)S(1)} %maximum_select_fusion.3), channel_id=1, source_target_pairs={{0,1},{1,0},{2,3},{3,2},{4,5},{5,4},{6,7},{7,6},{8,9},{9,8},{10,11... | collective-permute-start | bytes 2359304 | tf_op jit(solution)/shard_map/ppermute | solution.py:42
  74.5 38.6 %collective-permute-start.11 = (bf16[2,192,1024]{2,1,0:T(8,128)(2,1)S(1)}, bf16[2,192,1024]{2,1,0:T(8,128)(2,1)S(1)}, u32[]{:S(2)}, u32[]{:S(2)}) collective-permute-start(bf16[2,192,1024]{2,1,0:T(8,128)(2,1)S(1)} %maximum_select_fusion.5), channel_id=1, source_target_pairs={{0,4},{4,0},{1,5},{5,1},{2,6},{6,2},{3,7},{7,3},{8,12},{12,8},{9,1... | collective-permute-start | bytes 2359304 | tf_op jit(solution)/shard_map/ppermute | solution.py:42
  82.8 32.3 %collective-permute-start.3 = (bf16[272,1024]{1,0:T(8,128)(2,1)S(1)}, bf16[272,1024]{1,0:T(8,128)(2,1)S(1)}, u32[]{:S(2)}, u32[]{:S(2)}) collective-permute-start(bf16[272,1024]{1,0:T(8,128)(2,1)S(1)} %collective-permute-done.1), channel_id=1, source_target_pairs={{0,2},{2,0},{1,3},{3,1},{4,6},{6,4},{5,7},{7,5},{8,10},{10,8},{9,1... | collective-permute-start | bytes 1671176 | tf_op jit(solution)/shard_map/ppermute | solution.py:42
  108.5 10.4 %collective-permute-start.9 = (bf16[2,2,192,1024]{3,2,1,0:T(8,128)(2,1)}, bf16[2,2,192,1024]{3,2,1,0:T(8,128)(2,1)}, u32[]{:S(2)}, u32[]{:S(2)}) collective-permute-start(bf16[2,2,192,1024]{3,2,1,0:T(8,128)(2,1)} %maximum_select_fusion.1), channel_id=1, source_target_pairs={{0,2},{2,0},{1,3},{3,1},{4,6},{6,4},{5,7},{7,5},{8,10},{10,8},{9,1... | collective-permute-start | bytes 4718600 | tf_op jit(solution)/shard_map/ppermute | solution.py:42
  113.4 15.3 %collective-permute-start.12 = (bf16[2,2,192,1024]{3,2,1,0:T(8,128)(2,1)S(1)}, bf16[2,2,192,1024]{3,2,1,0:T(8,128)(2,1)}, u32[]{:S(2)}, u32[]{:S(2)}) collective-permute-start(bf16[2,2,192,1024]{3,2,1,0:T(8,128)(2,1)S(1)} %copy.124), channel_id=1, source_target_pairs={{0,2},{2,0},{1,3},{3,1},{4,6},{6,4},{5,7},{7,5},{8,10},{10,8},{9,1... | collective-permute-start | bytes 4718600 | tf_op jit(solution)/shard_map/ppermute | solution.py:42
  158.6 23.8 %collective-permute-start.14 = (bf16[256,1024]{1,0:T(8,128)(2,1)S(1)}, bf16[256,1024]{1,0:T(8,128)(2,1)}, u32[]{:S(2)}, u32[]{:S(2)}) collective-permute-start(bf16[256,1024]{1,0:T(8,128)(2,1)S(1)} %get-tuple-element.108), channel_id=1, source_target_pairs={{0,8},{8,0},{1,9},{9,1},{2,10},{10,2},{3,11},{11,3},{4,12},{12,4},... | collective-permute-start | bytes 1572872 | tf_op jit(solution)/shard_map/ppermute | solution.py:42
  165.6 28.0 %collective-permute-start.21 = (bf16[256,1024]{1,0:T(8,128)(2,1)}, bf16[256,1024]{1,0:T(8,128)(2,1)}, u32[]{:S(2)}, u32[]{:S(2)}) collective-permute-start(bf16[256,1024]{1,0:T(8,128)(2,1)} %bitcast.50), channel_id=1, source_target_pairs={{0,8},{8,0},{1,9},{9,1},{2,10},{10,2},{3,11},{11,3},{4,12},{12,4},... | collective-permute-start | bytes 1572872 | tf_op jit(solution)/shard_map/ppermute | solution.py:42
  165.7 28.1 %collective-permute-start.13 = (bf16[256,1024]{1,0:T(8,128)(2,1)S(1)}, bf16[256,1024]{1,0:T(8,128)(2,1)}, u32[]{:S(2)}, u32[]{:S(2)}) collective-permute-start(bf16[256,1024]{1,0:T(8,128)(2,1)S(1)} %get-tuple-element.108), channel_id=1, source_target_pairs={{0,2},{2,0},{1,3},{3,1},{4,6},{6,4},{5,7},{7,5},{8,10},{10,8},{9,1... | collective-permute-start | bytes 1572872 | tf_op jit(solution)/shard_map/ppermute | solution.py:42
  182.4 11.3 %collective-permute-start.15 = (bf16[256,1024]{1,0:T(8,128)(2,1)}, bf16[256,1024]{1,0:T(8,128)(2,1)}, u32[]{:S(2)}, u32[]{:S(2)}) collective-permute-start(bf16[256,1024]{1,0:T(8,128)(2,1)} %collective-permute-done.14), channel_id=1, source_target_pairs={{0,2},{2,0},{1,3},{3,1},{4,6},{6,4},{5,7},{7,5},{8,10},{10,8},{9,1... | collective-permute-start | bytes 1572872 | tf_op jit(solution)/shard_map/ppermute | solution.py:42
  182.5 30.8 %collective-permute-start.20 = (bf16[256,1024]{1,0:T(8,128)(2,1)}, bf16[256,1024]{1,0:T(8,128)(2,1)}, u32[]{:S(2)}, u32[]{:S(2)}) collective-permute-start(bf16[256,1024]{1,0:T(8,128)(2,1)} %bitcast.50), channel_id=1, source_target_pairs={{0,2},{2,0},{1,3},{3,1},{4,6},{6,4},{5,7},{7,5},{8,10},{10,8},{9,1... | collective-permute-start | bytes 1572872 | tf_op jit(solution)/shard_map/ppermute | solution.py:42
  193.6 19.7 %collective-permute-start.22 = (bf16[256,1024]{1,0:T(8,128)(2,1)}, bf16[256,1024]{1,0:T(8,128)(2,1)}, u32[]{:S(2)}, u32[]{:S(2)}) collective-permute-start(bf16[256,1024]{1,0:T(8,128)(2,1)} %collective-permute-done.21), channel_id=1, source_target_pairs={{0,2},{2,0},{1,3},{3,1},{4,6},{6,4},{5,7},{7,5},{8,10},{10,8},{9,1... | collective-permute-start | bytes 1572872 | tf_op jit(solution)/shard_map/ppermute | solution.py:42
  230.4 207.4 %reduce-scatter.3.cloned.1.call-start = ((), (), s32[]{:S(2)}) async-start(), calls=%async_computation.3 | async-start | bytes 5308416 | tf_op jit(solution)/shard_map/reduce_scatter | solution.py:481
  239.1 20.9 %collective-permute-start.18 = (bf16[512,1024]{1,0:T(8,128)(2,1)}, bf16[512,1024]{1,0:T(8,128)(2,1)}, u32[]{:S(2)}, u32[]{:S(2)}) collective-permute-start(bf16[512,1024]{1,0:T(8,128)(2,1)} %pad_maximum_fusion.9), channel_id=1, source_target_pairs={{0,2},{2,0},{1,3},{3,1},{4,6},{6,4},{5,7},{7,5},{8,10},{10,8},{9,1... | collective-permute-start | bytes 3145736 | tf_op jit(solution)/shard_map/ppermute | solution.py:42
  245.9 8.7 %collective-permute-start.23 = (bf16[512,1024]{1,0:T(8,128)(2,1)S(1)}, bf16[512,1024]{1,0:T(8,128)(2,1)S(1)}, u32[]{:S(2)}, u32[]{:S(2)}) collective-permute-start(bf16[512,1024]{1,0:T(8,128)(2,1)S(1)} %pad_maximum_fusion.10), channel_id=1, source_target_pairs={{0,2},{2,0},{1,3},{3,1},{4,6},{6,4},{5,7},{7,5},{8,10},{10,8},{9,1... | collective-permute-start | bytes 3145736 | tf_op jit(solution)/shard_map/ppermute | solution.py:42
  257.1 19.2 %collective-permute-start.24 = (bf16[256,1024]{1,0:T(8,128)(2,1)}, bf16[256,1024]{1,0:T(8,128)(2,1)S(1)}, u32[]{:S(2)}, u32[]{:S(2)}) collective-permute-start(bf16[256,1024]{1,0:T(8,128)(2,1)} %fusion.20), channel_id=1, source_target_pairs={{0,8},{8,0},{1,9},{9,1},{2,10},{10,2},{3,11},{11,3},{4,12},{12,4},... | collective-permute-start | bytes 1572872 | tf_op jit(solution)/shard_map/ppermute | solution.py:42
  265.2 187.2 %collective-permute-start.19 = (bf16[256,1024]{1,0:T(8,128)(2,1)}, bf16[256,1024]{1,0:T(8,128)(2,1)}, u32[]{:S(2)}, u32[]{:S(2)}) collective-permute-start(bf16[256,1024]{1,0:T(8,128)(2,1)} %fusion.22), channel_id=1, source_target_pairs={{0,8},{8,0},{1,9},{9,1},{2,10},{10,2},{3,11},{11,3},{4,12},{12,4},... | collective-permute-start | bytes 1572872 | tf_op jit(solution)/shard_map/ppermute | solution.py:42
  287.0 42.6 %collective-permute-start.37 = (bf16[8,64,1024]{2,1,0:T(8,128)(2,1)}, bf16[8,64,1024]{2,1,0:T(8,128)(2,1)}, u32[]{:S(2)}, u32[]{:S(2)}) collective-permute-start(bf16[8,64,1024]{2,1,0:T(8,128)(2,1)} %get-tuple-element.72), channel_id=1, source_target_pairs={{0,2},{2,0},{1,3},{3,1},{4,6},{6,4},{5,7},{7,5},{8,10},{10,8},{9,1... | collective-permute-start | bytes 3145736 | tf_op jit(solution)/shard_map/ppermute | solution.py:42
  316.6 58.8 %collective-permute-start.25 = (bf16[256,1024]{1,0:T(8,128)(2,1)}, bf16[256,1024]{1,0:T(8,128)(2,1)}, u32[]{:S(2)}, u32[]{:S(2)}) collective-permute-start(bf16[256,1024]{1,0:T(8,128)(2,1)} %get-tuple-element.118), channel_id=1, source_target_pairs={{0,2},{2,0},{1,3},{3,1},{4,6},{6,4},{5,7},{7,5},{8,10},{10,8},{9,1... | collective-permute-start | bytes 1572872 | tf_op jit(solution)/shard_map/ppermute | solution.py:42
  317.2 15.8 %collective-permute-start.26 = (bf16[256,1024]{1,0:T(8,128)(2,1)}, bf16[256,1024]{1,0:T(8,128)(2,1)}, u32[]{:S(2)}, u32[]{:S(2)}) collective-permute-start(bf16[256,1024]{1,0:T(8,128)(2,1)} %get-tuple-element.117), channel_id=1, source_target_pairs={{0,2},{2,0},{1,3},{3,1},{4,6},{6,4},{5,7},{7,5},{8,10},{10,8},{9,1... | collective-permute-start | bytes 1572872 | tf_op jit(solution)/shard_map/ppermute | solution.py:42
  328.3 59.0 %collective-permute-start.29 = (bf16[8,128,1024]{2,1,0:T(8,128)(2,1)}, bf16[8,128,1024]{2,1,0:T(8,128)(2,1)}, u32[]{:S(2)}, u32[]{:S(2)}) collective-permute-start(bf16[8,128,1024]{2,1,0:T(8,128)(2,1)} %get-tuple-element.69), channel_id=1, source_target_pairs={{0,2},{2,0},{1,3},{3,1},{4,6},{6,4},{5,7},{7,5},{8,10},{10,8},{9,1... | collective-permute-start | bytes 6291464 | tf_op jit(solution)/shard_map/ppermute | solution.py:42
  331.4 8.9 %collective-permute-start.40 = (bf16[2,2,64,512]{3,2,0,1:T(8,128)(2,1)S(1)}, bf16[2,2,64,512]{3,2,0,1:T(8,128)(2,1)S(1)}, u32[]{:S(2)}, u32[]{:S(2)}) collective-permute-start(bf16[2,2,64,512]{3,2,0,1:T(8,128)(2,1)S(1)} %broadcast_select_fusion.3), channel_id=1, source_target_pairs={{0,1},{1,0},{2,3},{3,2},{4,5},{5,4},{6,7},{7,6},{8,9},{9,8},{10,11... | collective-permute-start | bytes 786440 | tf_op jit(solution)/shard_map/ppermute | solution.py:42
  334.3 42.8 %collective-permute-start.27 = (bf16[256,1024]{1,0:T(8,128)(2,1)S(1)}, bf16[256,1024]{1,0:T(8,128)(2,1)S(1)}, u32[]{:S(2)}, u32[]{:S(2)}) collective-permute-start(bf16[256,1024]{1,0:T(8,128)(2,1)S(1)} %add_convert_fusion.3), channel_id=1, source_target_pairs={{0,4},{4,0},{1,5},{5,1},{2,6},{6,2},{3,7},{7,3},{8,12},{12,8},{9,1... | collective-permute-start | bytes 1572872 | tf_op jit(solution)/shard_map/ppermute | solution.py:42
  340.3 21.9 %collective-permute-start.38 = (bf16[2,64,1024]{2,1,0:T(8,128)(2,1)S(1)}, bf16[2,64,1024]{2,1,0:T(8,128)(2,1)S(1)}, u32[]{:S(2)}, u32[]{:S(2)}) collective-permute-start(bf16[2,64,1024]{2,1,0:T(8,128)(2,1)S(1)} %dynamic-slice_bitcast_fusion.1), channel_id=1, source_target_pairs={{0,4},{4,0},{1,5},{5,1},{2,6},{6,2},{3,7},{7,3},{8,12},{12,8},{9,1... | collective-permute-start | bytes 786440 | tf_op jit(solution)/shard_map/ppermute | solution.py:42
  367.1 7.5 %collective-permute-start.39 = (bf16[2,64,512]{2,1,0:T(8,128)(2,1)S(1)}, bf16[2,64,512]{2,1,0:T(8,128)(2,1)S(1)}, u32[]{:S(2)}, u32[]{:S(2)}) collective-permute-start(bf16[2,64,512]{2,1,0:T(8,128)(2,1)S(1)} %broadcast_select_fusion.5), channel_id=1, source_target_pairs={{0,1},{1,0},{2,3},{3,2},{4,5},{5,4},{6,7},{7,6},{8,9},{9,8},{10,11... | collective-permute-start | bytes 393224 | tf_op jit(solution)/shard_map/ppermute | solution.py:42
  375.5 7.7 %collective-permute-start.43 = (bf16[64,512]{1,0:T(8,128)(2,1)S(1)}, bf16[64,512]{1,0:T(8,128)(2,1)S(1)}, u32[]{:S(2)}, u32[]{:S(2)}) collective-permute-start(bf16[64,512]{1,0:T(8,128)(2,1)S(1)} %get-tuple-element.151), channel_id=1, source_target_pairs={{0,16},{8,24},{16,0},{24,8},{1,17},{9,25},{17,1},{25,9},{2,18},{10... | collective-permute-start | bytes 196616 | tf_op jit(solution)/shard_map/ppermute | solution.py:323
  381.6 12.7 %collective-permute-start.28 = (bf16[256,1024]{1,0:T(8,128)(2,1)}, bf16[256,1024]{1,0:T(8,128)(2,1)}, u32[]{:S(2)}, u32[]{:S(2)}) collective-permute-start(bf16[256,1024]{1,0:T(8,128)(2,1)} %fusion.19), channel_id=1, source_target_pairs={{8,0},{16,8},{24,16},{9,1},{17,9},{25,17},{10,2},{18,10},{26,18},{... | collective-permute-start | bytes 1572872 | tf_op jit(solution)/shard_map/ppermute | solution.py:76
  390.8 10.3 %collective-permute-start.30 = (bf16[2,128,1024]{2,1,0:T(8,128)(2,1)S(1)}, bf16[2,128,1024]{2,1,0:T(8,128)(2,1)S(1)}, u32[]{:S(2)}, u32[]{:S(2)}) collective-permute-start(bf16[2,128,1024]{2,1,0:T(8,128)(2,1)S(1)} %dynamic-slice_bitcast_fusion), channel_id=1, source_target_pairs={{0,4},{4,0},{1,5},{5,1},{2,6},{6,2},{3,7},{7,3},{8,12},{12,8},{9,1... | collective-permute-start | bytes 1572872 | tf_op jit(solution)/shard_map/ppermute | solution.py:42
  393.1 10.8 %collective-permute-start.32 = (bf16[2,2,128,512]{3,2,0,1:T(8,128)(2,1)S(1)}, bf16[2,2,128,512]{3,2,0,1:T(8,128)(2,1)S(1)}, u32[]{:S(2)}, u32[]{:S(2)}) collective-permute-start(bf16[2,2,128,512]{3,2,0,1:T(8,128)(2,1)S(1)} %broadcast_select_fusion.2), channel_id=1, source_target_pairs={{0,1},{1,0},{2,3},{3,2},{4,5},{5,4},{6,7},{7,6},{8,9},{9,8},{10,11... | collective-permute-start | bytes 1572872 | tf_op jit(solution)/shard_map/ppermute | solution.py:42
  401.4 6.9 %collective-permute-start.31 = (bf16[2,128,512]{2,1,0:T(8,128)(2,1)S(1)}, bf16[2,128,512]{2,1,0:T(8,128)(2,1)S(1)}, u32[]{:S(2)}, u32[]{:S(2)}) collective-permute-start(bf16[2,128,512]{2,1,0:T(8,128)(2,1)S(1)} %broadcast_select_fusion.4), channel_id=1, source_target_pairs={{0,1},{1,0},{2,3},{3,2},{4,5},{5,4},{6,7},{7,6},{8,9},{9,8},{10,11... | collective-permute-start | bytes 786440 | tf_op jit(solution)/shard_map/ppermute | solution.py:42
  410.0 9.8 %collective-permute-start.45 = (bf16[64,2,576]{2,0,1:T(8,128)(2,1)S(1)}, bf16[64,2,576]{2,0,1:T(8,128)(2,1)S(1)}, u32[]{:S(2)}, u32[]{:S(2)}) collective-permute-start(bf16[64,2,576]{2,0,1:T(8,128)(2,1)S(1)} %bitcast.297), channel_id=1, source_target_pairs={{0,2},{2,0},{1,3},{3,1},{4,6},{6,4},{5,7},{7,5},{8,10},{10,8},{9,1... | collective-permute-start | bytes 442376 | tf_op jit(solution)/shard_map/ppermute | solution.py:42
  413.6 11.3 %collective-permute-start.34 = (bf16[128,512]{1,0:T(8,128)(2,1)}, bf16[128,512]{1,0:T(8,128)(2,1)S(1)}, u32[]{:S(2)}, u32[]{:S(2)}) collective-permute-start(bf16[128,512]{1,0:T(8,128)(2,1)} %get-tuple-element.138), channel_id=1, source_target_pairs={{0,8},{8,16},{16,24},{24,0},{1,9},{9,17},{17,25},{25,1},{2,10},{10... | collective-permute-start | bytes 393224 | tf_op jit(solution)/shard_map/ppermute | solution.py:323
  416.8 9.8 %collective-permute-start.35 = (bf16[128,512]{1,0:T(8,128)(2,1)}, bf16[128,512]{1,0:T(8,128)(2,1)S(1)}, u32[]{:S(2)}, u32[]{:S(2)}) collective-permute-start(bf16[128,512]{1,0:T(8,128)(2,1)} %get-tuple-element.139), channel_id=1, source_target_pairs={{0,16},{8,24},{16,0},{24,8},{1,17},{9,25},{17,1},{25,9},{2,18},{10... | collective-permute-start | bytes 393224 | tf_op jit(solution)/shard_map/ppermute | solution.py:323
  419.2 8.0 %collective-permute-start.36 = (bf16[128,512]{1,0:T(8,128)(2,1)}, bf16[128,512]{1,0:T(8,128)(2,1)}, u32[]{:S(2)}, u32[]{:S(2)}) collective-permute-start(bf16[128,512]{1,0:T(8,128)(2,1)} %get-tuple-element.136), channel_id=1, source_target_pairs={{0,24},{8,0},{16,8},{24,16},{1,25},{9,1},{17,9},{25,17},{2,26},{10... | collective-permute-start | bytes 393224 | tf_op jit(solution)/shard_map/ppermute | solution.py:323
  420.5 11.3 %collective-permute-start.46 = (bf16[64,2304]{1,0:T(8,128)(2,1)S(1)}, bf16[64,2304]{1,0:T(8,128)(2,1)S(1)}, u32[]{:S(2)}, u32[]{:S(2)}) collective-permute-start(bf16[64,2304]{1,0:T(8,128)(2,1)S(1)} %reshape.413), channel_id=1, source_target_pairs={{0,0},{1,8},{8,1},{9,9},{2,2},{3,10},{10,3},{11,11},{4,4},{5,12},{... | collective-permute-start | bytes 884744 | tf_op jit(solution)/shard_map/ppermute | solution.py:488
  431.7 13.2 %collective-permute-start.52 = (f32[10,128]{1,0:T(8,128)S(1)}, f32[10,128]{1,0:T(8,128)S(1)}, u32[]{:S(2)}, u32[]{:S(2)}) collective-permute-start(f32[10,128]{1,0:T(8,128)S(1)} %pad_maximum_fusion.18), channel_id=1, source_target_pairs={{0,2},{2,0},{1,3},{3,1},{4,6},{6,4},{5,7},{7,5},{8,10},{10,8},{9,1... | collective-permute-start | bytes 15368 | tf_op jit(solution)/shard_map/ppermute | solution.py:93
  (75 other events, 614.9 us)
Sparse Core Ops, SparseCore 0:
  10.9 101.9 all-gather.5
  115.6 55.8 all-gather.3
  230.5 56.4 reduce-scatter.4
  291.0 93.1 reduce-scatter.2
where the time goes:
time: 492 us; the launch traced here: 483 us
  waiting for transfers between devices  134 us (27%)
  starting transfers between devices  93.5 us (19%)
  Pallas kernels  89.6 us (18%)
  matrix products  71.1 us (14%)
  other arithmetic  54.7 us (11%)
  local copies, waits for them, and re-layouts  20.4 us (4%)
  between operations  19.7 us (4%)
    ppermute x34, waiting for transfers between devices, swap(): return lax.ppermute(block, axis, [(0, 1), (1, 0)])  112 us
    ppermute x34, starting transfers between devices, swap(): return lax.ppermute(block, axis, [(0, 1), (1, 0)])  57.3 us
    dot_general x7, matrix products, dot_nt(): lax.dot_general(a, b, (((1,), (1,)), ((), ())), preferred_element_type=F32)  33.2 us
    dot_general x7, matrix products, dot_nn(): lax.dot_general(a, b, (((1,), (0,)), ((), ())), preferred_element_type=F32)  25.6 us
    pallas_call x1, Pallas kernels, attend_back(): pl.pallas_call(backward_kernel, grid=(micro, N_PAIRS), in_specs=[q_spec,...  24.8 us
    pallas_call x4, Pallas kernels, moments(): pl.pallas_call(functools.partial(moments_kernel, which, steps, len(parts)...  18.2 us
    pallas_call x2, Pallas kernels, weight_grad(): pl.pallas_call(functools.partial(grad_kernel, tuple(firsts)), grid_spec=p...  17.5 us
    ppermute x3, waiting for transfers between devices, far_blocks(): lax.ppermute(block, FAR, [(i, (i + distance) % size) for i in range(size)])  16 us
  transfers between devices with their start and end apart: 61, of which 23 were waited for; matrix products, arithmetic and copies ran while one was open for 23% of the time, Pallas kernels for 18%

commit v1 on v0

--- a/solution.py
+++ b/solution.py
@@ -352,32 +352,25 @@
 
         @pl.when(is_mine)
         def _(out=out, at=at):
-            out[0, 0] = mine_ref[0, at, :]
+            out[:, 0] = mine_ref[:, at, :]
 
         @pl.when(jnp.logical_not(is_mine))
         def _(out=out, at=at):
-            out[0, 0] = other_ref[0, at, :]
+            out[:, 0] = other_ref[:, at, :]
 
 
 def interleave(mine, other, k, widths):
     columns = mine.shape[-1]
     mine, other = (v.reshape(-1, sum(widths), columns) for v in (mine, other))
     count = mine.shape[0]
-
-    def block_of(core):
-        def index(c, i, k_ref):
-            wanted = k_ref[0] if core == 0 else 1 - k_ref[0]
-            return jnp.where(c == wanted, i, jnp.where(c < wanted, 0, count - 1)), 0, 0
-
-        return pl.BlockSpec((1, sum(widths), columns), index)
-
+    whole = pl.BlockSpec(mine.shape, lambda c, _: (0, 0, 0))
     outs = pl.pallas_call(
         interleave_kernel,
         grid_spec=pltpu.PrefetchScalarGridSpec(
             num_scalar_prefetch=1,
-            grid=(2, count),
-            in_specs=[block_of(0), block_of(1)],
-            out_specs=[pl.BlockSpec((1, 1, width, columns), lambda c, i, _: (i, c, 0, 0)) for width in widths],
+            grid=(2,),
+            in_specs=[whole, whole],
+            out_specs=[pl.BlockSpec((count, 1, width, columns), lambda c, _: (0, c, 0, 0)) for width in widths],
         ),
         out_shape=[jax.ShapeDtypeStruct((count, 2, width, columns), BF) for width in widths],
         cost_estimate=pl.CostEstimate(flops=0, bytes_accessed=8 * mine.size, transcendentals=0),
@@ -403,45 +396,48 @@
 def grad_kernel(firsts, k_ref, *refs):
     groups = len(firsts) - 1
     keep, leave = refs[2 * groups :]
-    width = keep.shape[1]
+    chips, width, _ = keep.shape
     for i in range(groups):
 
         @pl.when((pl.program_id(0) >= firsts[i]) & (pl.program_id(0) < firsts[i + 1]))
         def _(i=i):
             whole = dot_tn(refs[2 * i][...], refs[2 * i + 1][...])
             is_first = k_ref[0] == 0
-            keep[0] = jnp.where(is_first, whole[:width], whole[width:]).astype(BF)
-            leave[0] = jnp.where(is_first, whole[width:], whole[:width]).astype(BF)
+            for chip in range(chips):
+                at = 2 * chip * width
+                first, second = whole[at : at + width], whole[at + width : at + 2 * width]
+                keep[chip] = jnp.where(is_first, first, second).astype(BF)
+                leave[chip] = jnp.where(is_first, second, first).astype(BF)
 
 
 def weight_grad(pairs, k):
     chips = lax.axis_size(FAR) * lax.axis_size("near")
     chip_width = sum(a.shape[1] for a, _ in pairs) // chips
-    if chip_width % 128:
+    step = min(512, *(a.shape[1] for a, _ in pairs))
+    if chip_width % 128 or step % chip_width:
         whole = jnp.concatenate([dot_tn(a, b).astype(BF) for a, b in pairs])
         whole = whole.reshape(chips, 2, chip_width // 2, -1)
         return pick(whole, k, 1), pick(whole, 1 - k, 1)
     firsts, specs, operands = [0], [], []
     for a, b in pairs:
-        start, count = firsts[-1], a.shape[1] // chip_width
-        block = pl.BlockSpec(
-            (a.shape[0], chip_width), lambda i, _, s=start, c=count: (0, jnp.clip(i - s, 0, c - 1))
-        )
+        start, count = firsts[-1], a.shape[1] // step
+        block = pl.BlockSpec((a.shape[0], step), lambda i, _, s=start, c=count: (0, jnp.clip(i - s, 0, c - 1)))
         specs += [block, pl.BlockSpec(b.shape, lambda i, _: (0, 0))]
         operands += [a, b]
         firsts.append(start + count)
     columns = pairs[0][1].shape[1]
-    out = pl.BlockSpec((1, chip_width // 2, columns), lambda i, _: (i, 0, 0))
+    out = pl.BlockSpec((step // chip_width, chip_width // 2, columns), lambda i, _: (i, 0, 0))
     shape = jax.ShapeDtypeStruct((chips, chip_width // 2, columns), BF)
-    flops = sum(2 * a.shape[0] * a.shape[1] * columns for a, _ in pairs)
     return pl.pallas_call(
         functools.partial(grad_kernel, tuple(firsts)),
         grid_spec=pltpu.PrefetchScalarGridSpec(
-            num_scalar_prefetch=1, grid=(chips,), in_specs=specs, out_specs=[out, out]
+            num_scalar_prefetch=1, grid=(firsts[-1],), in_specs=specs, out_specs=[out, out]
         ),
         out_shape=[shape, shape],
         cost_estimate=pl.CostEstimate(
-            flops=flops, bytes_accessed=2 * sum(a.size + b.size for a, b in pairs) + 4 * chips * chip_width * columns, transcendentals=0
+            flops=sum(2 * a.shape[0] * a.shape[1] * columns for a, _ in pairs),
+            bytes_accessed=2 * sum(a.size + b.size for a, b in pairs) + 4 * chips * chip_width * columns,
+            transcendentals=0,
         ),
         name="weight_grad",
     )(k.reshape(1).astype(jnp.int32), *operands)
@@ -521,16 +517,16 @@
     return partial[:rows] + other[rows:] + across.astype(F32)
 
 
-def finish_kernel(early_ref, late_ref, m_ref, mean_ref, sq_ref, g_out, w_out, f_out, s_out, n_out, r_out):
+def finish_kernel(total_ref, m_ref, mean_ref, sq_ref, g_out, w_out, f_out, s_out, n_out, r_out):
     row = lax.broadcasted_iota(jnp.int32, (17, 128), 0)
     lane = lax.broadcasted_iota(jnp.int32, (17, 128), 1)
-    grad = jnp.concatenate([late_ref[0:8, :], early_ref[0:8, :], late_ref[9:10, :]], axis=0)
+    grad = total_ref[0:17, :]
     first, second, update = lamb_moments(grad, mean_ref[...], sq_ref[...])
     g_out[...] = grad
     f_out[...] = first
     s_out[...] = second
     master = m_ref[...]
-    squares = early_ref[8:9, :] + late_ref[8:9, :]
+    squares = total_ref[17:18, :]
     at = lax.broadcasted_iota(jnp.int32, (1, 128), 1)
     segment = jnp.where(row < 8, 0, jnp.where(row < 16, 1, jnp.where(lane < HEAD_WIDTH, 2, 3)))
     spot_row = lax.broadcasted_iota(jnp.int32, (2, 8), 0)
@@ -557,14 +553,14 @@
     w_out[...] = master - RATE * ratio_gain * update
 
 
-def finish(early, late, master, mean, square):
+def finish(total, master, mean, square):
     shaped = [v.reshape(17, 128) for v in (master, mean, square)]
     plane = jax.ShapeDtypeStruct((17, 128), F32)
     *gains, norms, ratios = pl.pallas_call(
         finish_kernel,
         out_shape=[plane] * 4 + [jax.ShapeDtypeStruct((2, 8), F32), jax.ShapeDtypeStruct((1, 128), F32)],
         name="finish",
-    )(early, late, *shaped)
+    )(total, *shaped)
     return [g.reshape(GAINS) for g in gains], norms, ratios[0]
 
 
@@ -688,7 +684,8 @@
     grad_two = four_sum(grad_two_part)
     upgate_parts = scatter_upgate(grad_gate, grad_upper, two_four)
     down_parts = scatter_down(dot_tn(cot_four, hidden_low).astype(BF), k)
-    block_out = (lax.optimization_barrier(middle) + four_sum(dot_nt(hidden_low, down_t))).astype(BF).reshape(tokens.shape)
+    out_part = dot_nt(hidden_low, down_t)
+    block_out = (lax.optimization_barrier(middle) + four_sum(out_part)).astype(BF).reshape(tokens.shape)
 
     grad_middle, ffn_rows = norm_back(middle, inv_two, ffn_gain, grad_two)
     grad_middle = grad_middle + cot_low.astype(F32)
@@ -713,20 +710,19 @@
     parts = (qkv_parts, proj_parts, upgate_parts, down_parts)
     means = (qkv_mean, proj_mean, upgate_mean, down_mean)
     squares = (qkv_square, proj_square, upgate_square, down_square)
-    moved = [moments(i, parts[i], means[i], squares[i], masters[i]) for i in range(4)]
+    moved = []
+    for i in range(4):
+        moved.append(moments(i, parts[i], means[i], squares[i], masters[i]))
     heads_row = head_rows[0:2, :HEAD_WIDTH] + head_rows[0:2, HEAD_WIDTH:]
-    early_row = moved[1][4] + moved[2][4] + moved[3][4]
-    early = jnp.concatenate([jnp.sum(ffn_rows, axis=0).reshape(8, 128), early_row])
-    late = jnp.concatenate([jnp.sum(attn_rows, axis=0).reshape(8, 128), moved[0][4], heads_row.reshape(1, 128)])
-    early, late = total_everywhere(early), total_everywhere(late)
-    early_norms = jnp.sqrt(early[8])
-    gain_outs, lamb_norms, ratios = finish(early, late, gain_master, gain_mean, gain_square)
+    sums_row = moved[0][4] + moved[1][4] + moved[2][4] + moved[3][4]
+    gain_rows = jnp.concatenate([jnp.sum(attn_rows, axis=0), jnp.sum(ffn_rows, axis=0)]).reshape(16, 128)
+    total = total_everywhere(jnp.concatenate([gain_rows, heads_row.reshape(1, 128), sums_row]))
+    gain_outs, lamb_norms, ratios = finish(total, gain_master, gain_mean, gain_square)
     gain_grad, gain_weight, gain_first, gain_second = gain_outs
     outs = [block_out, input_grad]
     for i in range(4):
-        ratio = ratios[0] if i == 0 else early_norms[i] / (early_norms[4 + i] + EPS_ADAM)
         grad, first, second, update, _ = moved[i]
-        outs += [grad, masters[i] - RATE * ratio * update, first, second]
+        outs += [grad, masters[i] - RATE * ratios[i] * update, first, second]
     return (*outs, gain_grad, gain_weight, gain_first, gain_second, lamb_norms)
 
 

time: 492 us -> 486 us (0.988)
  waiting for transfers between devices: 134 us -> 151 us
  starting transfers between devices: 93.5 us -> 81.3 us
  Pallas kernels: 89.6 us -> 79.3 us
    ppermute x34, waiting for transfers between devices: 112 us -> 120 us  [swap(): return lax.ppermute(block, axis, [(0, 1), (1, 0)])]
    ppermute x34, starting transfers between devices: 57.3 us -> 50.8 us  [swap(): return lax.ppermute(block, axis, [(0, 1), (1, 0)])]
    pallas_call x2, Pallas kernels: 13.1 us -> 7.66 us  [interleave(): pl.pallas_call(interleave_kernel, grid_spec=pltpu.PrefetchScalarGridSpec(...]
    ppermute x10 -> x5, starting transfers between devices: 12.8 us -> 7.69 us  [total_everywhere(): lax.ppermute(block, axis, [(i, i ^ step) for i in range(size)])]
    unnamed x131 -> x129, local copies, waits for them, and re-layouts: 9.17 us -> 10.7 us
  transfers between devices with their start and end apart: 61 -> 56, of which waited for: 23 -> 24; matrix products, arithmetic and copies ran while one was open for 23% -> 23% of each run, Pallas kernels for 18% -> 16%
where the time goes in v1:
time: 486 us; the launch traced here: 478 us
  waiting for transfers between devices  151 us (31%)
  starting transfers between devices  81.3 us (17%)
  Pallas kernels  79.3 us (16%)
  matrix products  71.3 us (15%)
  other arithmetic  54.3 us (11%)
  local copies, waits for them, and re-layouts  22.7 us (5%)
  between operations  17.9 us (4%)
    ppermute x34, waiting for transfers between devices, swap(): return lax.ppermute(block, axis, [(0, 1), (1, 0)])  120 us
    ppermute x34, starting transfers between devices, swap(): return lax.ppermute(block, axis, [(0, 1), (1, 0)])  50.8 us
    dot_general x7, matrix products, dot_nt(): lax.dot_general(a, b, (((1,), (1,)), ((), ())), preferred_element_type=F32)  33.4 us
    dot_general x7, matrix products, dot_nn(): lax.dot_general(a, b, (((1,), (0,)), ((), ())), preferred_element_type=F32)  25.6 us
    pallas_call x1, Pallas kernels, attend_back(): pl.pallas_call(backward_kernel, grid=(micro, N_PAIRS), in_specs=[q_spec,...  24.8 us
    pallas_call x4, Pallas kernels, moments(): pl.pallas_call(functools.partial(moments_kernel, which, steps, len(parts)...  18.2 us
    ppermute x3, waiting for transfers between devices, far_blocks(): lax.ppermute(block, FAR, [(i, (i + distance) % size) for i in range(size)])  16 us
    pallas_call x1, Pallas kernels, attend(): pl.pallas_call(forward_kernel, grid=(micro, N_PAIRS), in_specs=[q_spec, k...  14.4 us
  transfers between devices with their start and end apart: 56, of which 24 were waited for; matrix products, arithmetic and copies ran while one was open for 23% of the time, Pallas kernels for 16%

profile of v1, /device:TPU:0, one launch (start us, length us, event | category | flops | bytes accessed | tf_op | source)
XLA Modules:
  0.0 477.7 jit_solution(17753930001137150328)
XLA Ops:
  9.8 5.1 %collective-permute-start.4 = (bf16[192,512]{1,0:T(8,128)(2,1)S(1)}, bf16[192,512]{1,0:T(8,128)(2,1)S(1)}, u32[]{:S(2)}, u32[]{:S(2)}) collective-permute-start(bf16[192,512]{1,0:T(8,128)(2,1)S(1)} %pad_maximum_fusion.16), channel_id=1, source_target_pairs={{0,24},{8,0},{16,8},{24,16},{1,25},{9,1},{17,9},{25,17},{2,26},{10... | collective-permute-start | bytes 589832 | tf_op jit(solution)/shard_map/ppermute | solution.py:305
  17.4 4.4 collective-permute-start
  23.9 16.0 %collective-permute-done.5 = bf16[192,512]{1,0:T(8,128)(2,1)S(1)} collective-permute-done((bf16[192,512]{1,0:T(8,128)(2,1)S(1)}, bf16[192,512]{1,0:T(8,128)(2,1)S(1)}, u32[]{:S(2)}, u32[]{:S(2)}) %collective-permute-start.5) | collective-permute-done | bytes 196640 | tf_op jit(solution)/shard_map/ppermute | solution.py:305
  44.5 18.5 %collective-permute-start.10 = (bf16[2,192,512]{2,1,0:T(8,128)(2,1)}, bf16[2,192,512]{2,1,0:T(8,128)(2,1)S(1)}, u32[]{:S(2)}, u32[]{:S(2)}) collective-permute-start(bf16[2,192,512]{2,1,0:T(8,128)(2,1)} %get-tuple-element.141), channel_id=1, source_target_pairs={{0,1},{1,0},{2,3},{3,2},{4,5},{5,4},{6,7},{7,6},{8,9},{9,8},{10,11... | collective-permute-start | bytes 1179656 | tf_op jit(solution)/shard_map/ppermute | solution.py:42
  66.6 7.6 %collective-permute-start.8 = (bf16[2,2,192,512]{3,2,1,0:T(8,128)(2,1)S(1)}, bf16[2,2,192,512]{3,2,1,0:T(8,128)(2,1)S(1)}, u32[]{:S(2)}, u32[]{:S(2)}) collective-permute-start(bf16[2,2,192,512]{3,2,1,0:T(8,128)(2,1)S(1)} %maximum_select_fusion.3), channel_id=1, source_target_pairs={{0,1},{1,0},{2,3},{3,2},{4,5},{5,4},{6,7},{7,6},{8,9},{9,8},{10,11... | collective-permute-start | bytes 2359304 | tf_op jit(solution)/shard_map/ppermute | solution.py:42
  76.3 6.5 %collective-permute-done.1 = bf16[272,1024]{1,0:T(8,128)(2,1)S(1)} collective-permute-done((bf16[272,1024]{1,0:T(8,128)(2,1)S(1)}, bf16[272,1024]{1,0:T(8,128)(2,1)S(1)}, u32[]{:S(2)}, u32[]{:S(2)}) %collective-permute-start.1) | collective-permute-done | bytes 557088 | tf_op jit(solution)/shard_map/ppermute | solution.py:42
  82.9 23.9 %collective-permute-done.8 = bf16[2,2,192,512]{3,2,1,0:T(8,128)(2,1)S(1)} collective-permute-done((bf16[2,2,192,512]{3,2,1,0:T(8,128)(2,1)S(1)}, bf16[2,2,192,512]{3,2,1,0:T(8,128)(2,1)S(1)}, u32[]{:S(2)}, u32[]{:S(2)}) %collective-permute-start.8) | collective-permute-done | bytes 786464 | tf_op jit(solution)/shard_map/ppermute | solution.py:42
  108.5 4.5 collective-permute-done.11
  118.9 3.8 interleave.2
  122.7 3.4 fusion.99.q_ref
  126.1 3.8 interleave.3
  129.9 6.2 %fusion.100.k_ref.v_ref = f32[5,2,128,1024]{3,2,1,0:T(8,128)} fusion(bf16[5,2,128,1024]{3,2,1,0:T(8,128)(2,1)S(1)} %bitcast.267, bf16[1024,1024,1,1]{1,0,3,2:T(8,128)(2,1)} %bitcast.277), kind=kOutput, calls=%fused_computation.241 | convolution fusion | flops 2684354560 | bytes 9961472 | tf_op jit(solution)/shard_map/dot_general | solution.py:124
  136.2 14.4 %attend.1 = bf16[2,128,1024]{2,1,0:T(8,128)(2,1)} custom-call(f32[2,128,1024]{2,1,0:T(8,128)} %fusion.99.q_ref, f32[5,2,128,1024]{3,2,1,0:T(8,128)} %fusion.100.k_ref.v_ref, f32[5,2,128,1024]{3,2,1,0:T(8,128)} %fusion.100.k_ref.v_ref, f32[2,1,128]{2,1,0:T(1,128)} %bitcast.311, f32[2,5,128]{2,1,0:T(8,128)} %select_bitcast_fusion.4.ks_ref, ...), custom_call_target="tpu_custom_call" | custom-call | flops 5368709120 | bytes 6815744 | tf_op jit(solution)/shard_map/attend/pallas_call | solution.py:268
  153.4 6.7 %collective-permute-start.14 = (bf16[256,1024]{1,0:T(8,128)(2,1)S(1)}, bf16[256,1024]{1,0:T(8,128)(2,1)}, u32[]{:S(2)}, u32[]{:S(2)}) collective-permute-start(bf16[256,1024]{1,0:T(8,128)(2,1)S(1)} %get-tuple-element.108), channel_id=1, source_target_pairs={{0,8},{8,0},{1,9},{9,1},{2,10},{10,2},{3,11},{11,3},{4,12},{12,4},... | collective-permute-start | bytes 1572872 | tf_op jit(solution)/shard_map/ppermute | solution.py:42
  160.4 19.7 %collective-permute-done.14 = bf16[256,1024]{1,0:T(8,128)(2,1)} collective-permute-done((bf16[256,1024]{1,0:T(8,128)(2,1)S(1)}, bf16[256,1024]{1,0:T(8,128)(2,1)}, u32[]{:S(2)}, u32[]{:S(2)}) %collective-permute-start.14) | collective-permute-done | bytes 524320 | tf_op jit(solution)/shard_map/ppermute | solution.py:42
  180.6 10.6 %collective-permute-done.21 = bf16[256,1024]{1,0:T(8,128)(2,1)} collective-permute-done((bf16[256,1024]{1,0:T(8,128)(2,1)}, bf16[256,1024]{1,0:T(8,128)(2,1)}, u32[]{:S(2)}, u32[]{:S(2)}) %collective-permute-start.21) | collective-permute-done | bytes 524320 | tf_op jit(solution)/shard_map/ppermute | solution.py:42
  191.3 2.8 pad_maximum_fusion.3
  194.1 2.6 slice_bitcast_fusion.3
  196.8 7.6 %fusion.10 = f32[1024,1152]{1,0:T(8,128)} fusion(bf16[1152,512]{1,0:T(8,128)(2,1)S(1)} %get-tuple-element.116, bf16[1152,512]{1,0:T(8,128)(2,1)S(1)} %get-tuple-element.113, bf16[256,1024]{1,0:T(8,128)(2,1)} %collective-permute-done.15, bf16[256,1024]{1,0:T(8,128)(2,1)} %collective-permute-done.14, bf16[256,1024]{1,0:T(8,128)(2,1)} %collective-permute-done.13, ...), kind=kOutput, calls=%fused_computation.40 | convolution fusion | flops 2429026304 | bytes 9175040 | tf_op jit(solution)/shard_map/dot_general | solution.py:124
  204.4 6.4 %fusion.8 = f32[1024,1152]{1,0:T(8,128)} fusion(bf16[1152,512]{1,0:T(8,128)(2,1)S(1)} %get-tuple-element.114, bf16[1152,512]{1,0:T(8,128)(2,1)S(1)} %get-tuple-element.115, bf16[256,1024]{1,0:T(8,128)(2,1)} %collective-permute-done.15, bf16[256,1024]{1,0:T(8,128)(2,1)} %collective-permute-done.14, bf16[256,1024]{1,0:T(8,128)(2,1)} %collective-permute-done.13, ...), kind=kOutput, calls=%fused_computation.38 | convolution fusion | flops 2429026304 | bytes 9175040 | tf_op jit(solution)/shard_map/dot_general | solution.py:124
  210.8 10.4 %multiply_convert_fusion = (bf16[1024,1152]{1,0:T(8,128)(2,1)}, bf16[1024,1152]{1,0:T(8,128)(2,1)}, bf16[1024,1152]{1,0:T(8,128)(2,1)S(1)}) fusion(f32[1024,1152]{1,0:T(8,128)} %fusion.10, f32[1024,1152]{1,0:T(8,128)} %fusion.8, bf16[1024,1152]{1,0:T(8,128)(2,1)} %all-gather.4.cloned.1.call-done, bf16[256,1024]{1,0:T(8,128)(2,1)} %collective-permute-done.22, ...), kind=kOutput, calls=%fused_computation.6 | convolution fusion | flops 2442002432 | bytes 20971520 | tf_op jit(solution)/shard_map/dot_general | solution.py:132
  221.2 6.7 %convolution_convert_fusion = bf16[1024,1152]{1,0:T(8,128)(2,1)} fusion(bf16[1024,1152]{1,0:T(8,128)(2,1)S(1)} %get-tuple-element.112, bf16[256,1024]{1,0:T(8,128)(2,1)} %collective-permute-done.22, bf16[256,1024]{1,0:T(8,128)(2,1)} %collective-permute-done.21, bf16[256,1024]{1,0:T(8,128)(2,1)} %collective-permute-done.20, bf16[256,1024]{1,0:T(8,128)(2,1)} %bitcast.50), kind=kOutput, calls=%fused_computation.12 | convolution fusion | flops 2425487360 | bytes 6815744 | tf_op jit(solution)/shard_map/dot_general | solution.py:128
  228.0 7.5 %fusion.97 = (bf16[1024,1024]{1,0:T(8,128)(2,1)S(1)}, f32[1024,1024]{1,0:T(8,128)}) fusion(bf16[1024,1152]{1,0:T(8,128)(2,1)} %copy-done.60, bf16[1024,1152]{1,0:T(8,128)(2,1)} %all-gather.4.cloned.1.call-done), kind=kOutput, calls=%fused_computation.238 | convolution fusion | flops 2416967680 | bytes 11010048 | tf_op jit(solution)/shard_map/dot_general | solution.py:124
  237.5 2.9 fusion.9
  240.4 2.9 fusion.98
  254.7 2.9 pad_maximum_fusion
  264.8 9.1 %collective-permute-done.24 = bf16[256,1024]{1,0:T(8,128)(2,1)S(1)} collective-permute-done((bf16[256,1024]{1,0:T(8,128)(2,1)}, bf16[256,1024]{1,0:T(8,128)(2,1)S(1)}, u32[]{:S(2)}, u32[]{:S(2)}) %collective-permute-start.24) | collective-permute-done | bytes 524320 | tf_op jit(solution)/shard_map/ppermute | solution.py:42
  278.2 3.2 weight_grad.3
  284.0 24.8 %attend_back.1 = (bf16[2,128,1024]{2,1,0:T(8,128)(2,1)}, bf16[5,2,128,512]{3,2,1,0:T(8,128)(2,1)}, bf16[5,2,128,512]{3,2,1,0:T(8,128)(2,1)}, f32[8,128]{1,0:T(8,128)}) custom-call(f32[2,128,1024]{2,1,0:T(8,128)} %fusion.99.q_ref, f32[5,2,128,1024]{3,2,1,0:T(8,128)} %fusion.100.k_ref.v_ref, f32[5,2,128,1024]{3,2,1,0:T(8,128)} %fusion.100.k_ref.v_ref, ...), custom_call_target="tpu_custom_call" | custom-call | flops 13421772800 | bytes 6815744 | tf_op jit(solution)/shard_map/attend_back/pallas_call | solution.py:283
  311.6 9.5 %weight_grad.2 = (bf16[8,128,1024]{2,1,0:T(8,128)(2,1)}, bf16[8,128,1024]{2,1,0:T(8,128)(2,1)}) custom-call(s32[1]{0:T(128)} %bitcast.3.k_ref, bf16[256,1024]{1,0:T(8,128)(2,1)} %bitcast.292, bf16[256,1024]{1,0:T(8,128)(2,1)} %copy-done.22, bf16[1280,512]{1,0:T(8,128)(2,1)} %bitcast.241, bf16[1280,1024]{1,0:T(8,128)(2,1)} %copy-done.18, ...), custom_call_target="tpu_custom_call" | custom-call | flops 3221225472 | bytes 17301504 | tf_op jit(solution)/shard_map/weight_grad/pallas_call | solution.py:431
  328.5 6.8 %collective-permute-done.40 = bf16[2,2,64,512]{3,2,0,1:T(8,128)(2,1)S(1)} collective-permute-done((bf16[2,2,64,512]{3,2,0,1:T(8,128)(2,1)S(1)}, bf16[2,2,64,512]{3,2,0,1:T(8,128)(2,1)S(1)}, u32[]{:S(2)}, u32[]{:S(2)}) %collective-permute-start.40) | collective-permute-done | bytes 262176 | tf_op jit(solution)/shard_map/ppermute | solution.py:42
  336.8 19.2 %collective-permute-done.38 = bf16[2,64,1024]{2,1,0:T(8,128)(2,1)S(1)} collective-permute-done((bf16[2,64,1024]{2,1,0:T(8,128)(2,1)S(1)}, bf16[2,64,1024]{2,1,0:T(8,128)(2,1)S(1)}, u32[]{:S(2)}, u32[]{:S(2)}) %collective-permute-start.38) | collective-permute-done | bytes 262176 | tf_op jit(solution)/shard_map/ppermute | solution.py:42
  357.6 3.4 collective-permute-done.41
  361.1 5.6 %collective-permute-done.39 = bf16[2,64,512]{2,1,0:T(8,128)(2,1)S(1)} collective-permute-done((bf16[2,64,512]{2,1,0:T(8,128)(2,1)S(1)}, bf16[2,64,512]{2,1,0:T(8,128)(2,1)S(1)}, u32[]{:S(2)}, u32[]{:S(2)}) %collective-permute-start.39) | collective-permute-done | bytes 131104 | tf_op jit(solution)/shard_map/ppermute | solution.py:42
  367.5 3.9 collective-permute-start.44
  378.1 3.4 moments.5
  381.5 3.3 add_convert_fusion
  390.5 3.0 fusion.41
  393.5 5.6 %collective-permute-done.30 = bf16[2,128,1024]{2,1,0:T(8,128)(2,1)S(1)} collective-permute-done((bf16[2,128,1024]{2,1,0:T(8,128)(2,1)S(1)}, bf16[2,128,1024]{2,1,0:T(8,128)(2,1)S(1)}, u32[]{:S(2)}, u32[]{:S(2)}) %collective-permute-start.30) | collective-permute-done | bytes 524320 | tf_op jit(solution)/shard_map/ppermute | solution.py:42
  402.6 4.3 collective-permute-done.31
  411.1 3.3 collective-permute-start.34
  418.2 3.8 fusion.35
  424.9 3.8 moments.4
  429.5 5.4 %moments.7 = (f32[64,2304]{1,0:T(8,128)}, f32[64,2304]{1,0:T(8,128)}, f32[64,2304]{1,0:T(8,128)}, f32[64,2304]{1,0:T(8,128)}, f32[1,128]{1,0:T(1,128)}) custom-call(bf16[64,2304]{1,0:T(8,128)(2,1)} %copy-done.43, f32[64,2304]{1,0:T(8,128)} %bitcast.289, f32[64,2304]{1,0:T(8,128)} %bitcast.290, f32[64,2304]{1,0:T(8,128)} %bitcast.256), custom_call_target="tpu_custom_call" | custom-call | flops 2949120 | bytes 4718592 | tf_op jit(solution)/shard_map/moments/pallas_call | solution.py:609
  434.9 5.6 %moments.6 = (f32[576,512]{1,0:T(8,128)}, f32[576,512]{1,0:T(8,128)}, f32[576,512]{1,0:T(8,128)}, f32[576,512]{1,0:T(8,128)}, f32[1,128]{1,0:T(1,128)}) custom-call(bf16[576,512]{1,0:T(8,128)(2,1)} %bitcast.291, f32[576,512]{1,0:T(8,128)} %bitcast.284, f32[576,512]{1,0:T(8,128)} %bitcast.285, f32[576,512]{1,0:T(8,128)} %bitcast.251), custom_call_target="tpu_custom_call" | custom-call | flops 5898240 | bytes 9437184 | tf_op jit(solution)/shard_map/moments/pallas_call | solution.py:609
  442.7 3.2 collective-permute-start.48
  449.1 2.8 fusion.25
  453.0 3.7 collective-permute-done.50
  (340 shorter events, 115.1 us)
Async XLA Ops:
  7.3 186.9 %all-gather.6.cloned.1.call-start = ((), (), s32[]{:S(2)}) async-start(), calls=%async_computation.5 | async-start | bytes 5308416 | tf_op jit(solution)/shard_map/all_gather | solution.py:467
  9.6 201.2 %all-gather.4.cloned.1.call-start = ((), (), s32[]{:S(2)}) async-start(), calls=%async_computation.2 | async-start | bytes 2654208 | tf_op jit(solution)/shard_map/all_gather | solution.py:493
  9.8 14.1 %collective-permute-start.4 = (bf16[192,512]{1,0:T(8,128)(2,1)S(1)}, bf16[192,512]{1,0:T(8,128)(2,1)S(1)}, u32[]{:S(2)}, u32[]{:S(2)}) collective-permute-start(bf16[192,512]{1,0:T(8,128)(2,1)S(1)} %pad_maximum_fusion.16), channel_id=1, source_target_pairs={{0,24},{8,0},{16,8},{24,16},{1,25},{9,1},{17,9},{25,17},{2,26},{10... | collective-permute-start | bytes 589832 | tf_op jit(solution)/shard_map/ppermute | solution.py:305
  14.9 25.0 %collective-permute-start.5 = (bf16[192,512]{1,0:T(8,128)(2,1)S(1)}, bf16[192,512]{1,0:T(8,128)(2,1)S(1)}, u32[]{:S(2)}, u32[]{:S(2)}) collective-permute-start(bf16[192,512]{1,0:T(8,128)(2,1)S(1)} %pad_maximum_fusion.16), channel_id=1, source_target_pairs={{0,16},{8,24},{16,0},{24,8},{1,17},{9,25},{17,1},{25,9},{2,18},{10... | collective-permute-start | bytes 589832 | tf_op jit(solution)/shard_map/ppermute | solution.py:305
  14.9 25.0 %collective-permute-start.6 = (bf16[192,512]{1,0:T(8,128)(2,1)S(1)}, bf16[192,512]{1,0:T(8,128)(2,1)S(1)}, u32[]{:S(2)}, u32[]{:S(2)}) collective-permute-start(bf16[192,512]{1,0:T(8,128)(2,1)S(1)} %pad_maximum_fusion.16), channel_id=1, source_target_pairs={{0,8},{8,16},{16,24},{24,0},{1,9},{9,17},{17,25},{25,1},{2,10},{10... | collective-permute-start | bytes 589832 | tf_op jit(solution)/shard_map/ppermute | solution.py:305
  17.4 47.2 %collective-permute-start = (bf16[272,1024]{1,0:T(8,128)(2,1)}, bf16[272,1024]{1,0:T(8,128)(2,1)S(1)}, u32[]{:S(2)}, u32[]{:S(2)}) collective-permute-start(bf16[272,1024]{1,0:T(8,128)(2,1)} %fusion.40), channel_id=1, source_target_pairs={{0,8},{8,16},{16,24},{1,9},{9,17},{17,25},{2,10},{10,18},{18,26},{... | collective-permute-start | bytes 1671176 | tf_op jit(solution)/shard_map/ppermute | solution.py:55
  21.8 18.4 %collective-permute-start.16 = (bf16[64,2304]{1,0:T(8,128)(2,1)S(1)}, bf16[64,2304]{1,0:T(8,128)(2,1)S(1)}, u32[]{:S(2)}, u32[]{:S(2)}) collective-permute-start(bf16[64,2304]{1,0:T(8,128)(2,1)S(1)} %convert_bitcast_fusion.1), channel_id=1, source_target_pairs={{0,0},{1,8},{8,1},{9,9},{2,2},{3,10},{10,3},{11,11},{4,4},{5,12},{... | collective-permute-start | bytes 884744 | tf_op jit(solution)/shard_map/ppermute | solution.py:484
  41.3 21.7 %collective-permute-start.17 = (bf16[64,2,576]{2,0,1:T(8,128)(2,1)S(1)}, bf16[64,2,576]{2,0,1:T(8,128)(2,1)S(1)}, u32[]{:S(2)}, u32[]{:S(2)}) collective-permute-start(bf16[64,2,576]{2,0,1:T(8,128)(2,1)S(1)} %bitcast.298), channel_id=1, source_target_pairs={{0,2},{2,0},{1,3},{3,1},{4,6},{6,4},{5,7},{7,5},{8,10},{10,8},{9,1... | collective-permute-start | bytes 442376 | tf_op jit(solution)/shard_map/ppermute | solution.py:42
  42.2 23.2 %collective-permute-start.7 = (bf16[2,192,512]{2,1,0:T(8,128)(2,1)}, bf16[2,192,512]{2,1,0:T(8,128)(2,1)}, u32[]{:S(2)}, u32[]{:S(2)}) collective-permute-start(bf16[2,192,512]{2,1,0:T(8,128)(2,1)} %get-tuple-element.143), channel_id=1, source_target_pairs={{0,4},{4,0},{1,5},{5,1},{2,6},{6,2},{3,7},{7,3},{8,12},{12,8},{9,1... | collective-permute-start | bytes 1179656 | tf_op jit(solution)/shard_map/ppermute | solution.py:42
  44.5 29.8 %collective-permute-start.10 = (bf16[2,192,512]{2,1,0:T(8,128)(2,1)}, bf16[2,192,512]{2,1,0:T(8,128)(2,1)S(1)}, u32[]{:S(2)}, u32[]{:S(2)}) collective-permute-start(bf16[2,192,512]{2,1,0:T(8,128)(2,1)} %get-tuple-element.141), channel_id=1, source_target_pairs={{0,1},{1,0},{2,3},{3,2},{4,5},{5,4},{6,7},{7,6},{8,9},{9,8},{10,11... | collective-permute-start | bytes 1179656 | tf_op jit(solution)/shard_map/ppermute | solution.py:42
  64.5 342.5 %reduce-scatter.5.cloned.1.call-start = ((), (), s32[]{:S(2)}) async-start(), calls=%async_computation.4 | async-start | bytes 2654208 | tf_op jit(solution)/shard_map/reduce_scatter | solution.py:500
  64.8 18.0 %collective-permute-start.1 = (bf16[272,1024]{1,0:T(8,128)(2,1)S(1)}, bf16[272,1024]{1,0:T(8,128)(2,1)S(1)}, u32[]{:S(2)}, u32[]{:S(2)}) collective-permute-start(bf16[272,1024]{1,0:T(8,128)(2,1)S(1)} %get-tuple-element.126), channel_id=1, source_target_pairs={{0,4},{4,0},{1,5},{5,1},{2,6},{6,2},{3,7},{7,3},{8,12},{12,8},{9,1... | collective-permute-start | bytes 1671176 | tf_op jit(solution)/shard_map/ppermute | solution.py:42
  65.3 17.5 %collective-permute-start.2 = (bf16[272,1024]{1,0:T(8,128)(2,1)S(1)}, bf16[272,1024]{1,0:T(8,128)(2,1)S(1)}, u32[]{:S(2)}, u32[]{:S(2)}) collective-permute-start(bf16[272,1024]{1,0:T(8,128)(2,1)S(1)} %get-tuple-element.125), channel_id=1, source_target_pairs={{0,2},{2,0},{1,3},{3,1},{4,6},{6,4},{5,7},{7,5},{8,10},{10,8},{9,1... | collective-permute-start | bytes 1671176 | tf_op jit(solution)/shard_map/ppermute | solution.py:42
  66.6 40.2 %collective-permute-start.8 = (bf16[2,2,192,512]{3,2,1,0:T(8,128)(2,1)S(1)}, bf16[2,2,192,512]{3,2,1,0:T(8,128)(2,1)S(1)}, u32[]{:S(2)}, u32[]{:S(2)}) collective-permute-start(bf16[2,2,192,512]{3,2,1,0:T(8,128)(2,1)S(1)} %maximum_select_fusion.3), channel_id=1, source_target_pairs={{0,1},{1,0},{2,3},{3,2},{4,5},{5,4},{6,7},{7,6},{8,9},{9,8},{10,11... | collective-permute-start | bytes 2359304 | tf_op jit(solution)/shard_map/ppermute | solution.py:42
  74.5 38.6 %collective-permute-start.11 = (bf16[2,192,1024]{2,1,0:T(8,128)(2,1)S(1)}, bf16[2,192,1024]{2,1,0:T(8,128)(2,1)S(1)}, u32[]{:S(2)}, u32[]{:S(2)}) collective-permute-start(bf16[2,192,1024]{2,1,0:T(8,128)(2,1)S(1)} %maximum_select_fusion.5), channel_id=1, source_target_pairs={{0,4},{4,0},{1,5},{5,1},{2,6},{6,2},{3,7},{7,3},{8,12},{12,8},{9,1... | collective-permute-start | bytes 2359304 | tf_op jit(solution)/shard_map/ppermute | solution.py:42
  82.8 32.3 %collective-permute-start.3 = (bf16[272,1024]{1,0:T(8,128)(2,1)S(1)}, bf16[272,1024]{1,0:T(8,128)(2,1)S(1)}, u32[]{:S(2)}, u32[]{:S(2)}) collective-permute-start(bf16[272,1024]{1,0:T(8,128)(2,1)S(1)} %collective-permute-done.1), channel_id=1, source_target_pairs={{0,2},{2,0},{1,3},{3,1},{4,6},{6,4},{5,7},{7,5},{8,10},{10,8},{9,1... | collective-permute-start | bytes 1671176 | tf_op jit(solution)/shard_map/ppermute | solution.py:42
  108.5 10.4 %collective-permute-start.9 = (bf16[2,2,192,1024]{3,2,1,0:T(8,128)(2,1)}, bf16[2,2,192,1024]{3,2,1,0:T(8,128)(2,1)}, u32[]{:S(2)}, u32[]{:S(2)}) collective-permute-start(bf16[2,2,192,1024]{3,2,1,0:T(8,128)(2,1)} %maximum_select_fusion.1), channel_id=1, source_target_pairs={{0,2},{2,0},{1,3},{3,1},{4,6},{6,4},{5,7},{7,5},{8,10},{10,8},{9,1... | collective-permute-start | bytes 4718600 | tf_op jit(solution)/shard_map/ppermute | solution.py:42
  113.4 12.7 %collective-permute-start.12 = (bf16[2,2,192,1024]{3,2,1,0:T(8,128)(2,1)S(1)}, bf16[2,2,192,1024]{3,2,1,0:T(8,128)(2,1)}, u32[]{:S(2)}, u32[]{:S(2)}) collective-permute-start(bf16[2,2,192,1024]{3,2,1,0:T(8,128)(2,1)S(1)} %copy.124), channel_id=1, source_target_pairs={{0,2},{2,0},{1,3},{3,1},{4,6},{6,4},{5,7},{7,5},{8,10},{10,8},{9,1... | collective-permute-start | bytes 4718600 | tf_op jit(solution)/shard_map/ppermute | solution.py:42
  153.4 26.7 %collective-permute-start.14 = (bf16[256,1024]{1,0:T(8,128)(2,1)S(1)}, bf16[256,1024]{1,0:T(8,128)(2,1)}, u32[]{:S(2)}, u32[]{:S(2)}) collective-permute-start(bf16[256,1024]{1,0:T(8,128)(2,1)S(1)} %get-tuple-element.108), channel_id=1, source_target_pairs={{0,8},{8,0},{1,9},{9,1},{2,10},{10,2},{3,11},{11,3},{4,12},{12,4},... | collective-permute-start | bytes 1572872 | tf_op jit(solution)/shard_map/ppermute | solution.py:42
  160.1 31.1 %collective-permute-start.21 = (bf16[256,1024]{1,0:T(8,128)(2,1)}, bf16[256,1024]{1,0:T(8,128)(2,1)}, u32[]{:S(2)}, u32[]{:S(2)}) collective-permute-start(bf16[256,1024]{1,0:T(8,128)(2,1)} %bitcast.50), channel_id=1, source_target_pairs={{0,8},{8,0},{1,9},{9,1},{2,10},{10,2},{3,11},{11,3},{4,12},{12,4},... | collective-permute-start | bytes 1572872 | tf_op jit(solution)/shard_map/ppermute | solution.py:42
  160.2 31.1 %collective-permute-start.13 = (bf16[256,1024]{1,0:T(8,128)(2,1)S(1)}, bf16[256,1024]{1,0:T(8,128)(2,1)}, u32[]{:S(2)}, u32[]{:S(2)}) collective-permute-start(bf16[256,1024]{1,0:T(8,128)(2,1)S(1)} %get-tuple-element.108), channel_id=1, source_target_pairs={{0,2},{2,0},{1,3},{3,1},{4,6},{6,4},{5,7},{7,5},{8,10},{10,8},{9,1... | collective-permute-start | bytes 1572872 | tf_op jit(solution)/shard_map/ppermute | solution.py:42
  180.1 11.2 %collective-permute-start.15 = (bf16[256,1024]{1,0:T(8,128)(2,1)}, bf16[256,1024]{1,0:T(8,128)(2,1)}, u32[]{:S(2)}, u32[]{:S(2)}) collective-permute-start(bf16[256,1024]{1,0:T(8,128)(2,1)} %collective-permute-done.14), channel_id=1, source_target_pairs={{0,2},{2,0},{1,3},{3,1},{4,6},{6,4},{5,7},{7,5},{8,10},{10,8},{9,1... | collective-permute-start | bytes 1572872 | tf_op jit(solution)/shard_map/ppermute | solution.py:42
  180.1 30.7 %collective-permute-start.20 = (bf16[256,1024]{1,0:T(8,128)(2,1)}, bf16[256,1024]{1,0:T(8,128)(2,1)}, u32[]{:S(2)}, u32[]{:S(2)}) collective-permute-start(bf16[256,1024]{1,0:T(8,128)(2,1)} %bitcast.50), channel_id=1, source_target_pairs={{0,2},{2,0},{1,3},{3,1},{4,6},{6,4},{5,7},{7,5},{8,10},{10,8},{9,1... | collective-permute-start | bytes 1572872 | tf_op jit(solution)/shard_map/ppermute | solution.py:42
  191.3 19.5 %collective-permute-start.22 = (bf16[256,1024]{1,0:T(8,128)(2,1)}, bf16[256,1024]{1,0:T(8,128)(2,1)}, u32[]{:S(2)}, u32[]{:S(2)}) collective-permute-start(bf16[256,1024]{1,0:T(8,128)(2,1)} %collective-permute-done.21), channel_id=1, source_target_pairs={{0,2},{2,0},{1,3},{3,1},{4,6},{6,4},{5,7},{7,5},{8,10},{10,8},{9,1... | collective-permute-start | bytes 1572872 | tf_op jit(solution)/shard_map/ppermute | solution.py:42
  227.9 207.0 %reduce-scatter.3.cloned.1.call-start = ((), (), s32[]{:S(2)}) async-start(), calls=%async_computation.3 | async-start | bytes 5308416 | tf_op jit(solution)/shard_map/reduce_scatter | solution.py:477
  236.6 21.0 %collective-permute-start.18 = (bf16[512,1024]{1,0:T(8,128)(2,1)}, bf16[512,1024]{1,0:T(8,128)(2,1)}, u32[]{:S(2)}, u32[]{:S(2)}) collective-permute-start(bf16[512,1024]{1,0:T(8,128)(2,1)} %pad_maximum_fusion.9), channel_id=1, source_target_pairs={{0,2},{2,0},{1,3},{3,1},{4,6},{6,4},{5,7},{7,5},{8,10},{10,8},{9,1... | collective-permute-start | bytes 3145736 | tf_op jit(solution)/shard_map/ppermute | solution.py:42
  243.4 8.7 %collective-permute-start.23 = (bf16[512,1024]{1,0:T(8,128)(2,1)S(1)}, bf16[512,1024]{1,0:T(8,128)(2,1)S(1)}, u32[]{:S(2)}, u32[]{:S(2)}) collective-permute-start(bf16[512,1024]{1,0:T(8,128)(2,1)S(1)} %pad_maximum_fusion.10), channel_id=1, source_target_pairs={{0,2},{2,0},{1,3},{3,1},{4,6},{6,4},{5,7},{7,5},{8,10},{10,8},{9,1... | collective-permute-start | bytes 3145736 | tf_op jit(solution)/shard_map/ppermute | solution.py:42
  254.7 19.2 %collective-permute-start.24 = (bf16[256,1024]{1,0:T(8,128)(2,1)}, bf16[256,1024]{1,0:T(8,128)(2,1)S(1)}, u32[]{:S(2)}, u32[]{:S(2)}) collective-permute-start(bf16[256,1024]{1,0:T(8,128)(2,1)} %fusion.20), channel_id=1, source_target_pairs={{0,8},{8,0},{1,9},{9,1},{2,10},{10,2},{3,11},{11,3},{4,12},{12,4},... | collective-permute-start | bytes 1572872 | tf_op jit(solution)/shard_map/ppermute | solution.py:42
  262.8 186.4 %collective-permute-start.19 = (bf16[256,1024]{1,0:T(8,128)(2,1)}, bf16[256,1024]{1,0:T(8,128)(2,1)}, u32[]{:S(2)}, u32[]{:S(2)}) collective-permute-start(bf16[256,1024]{1,0:T(8,128)(2,1)} %fusion.22), channel_id=1, source_target_pairs={{0,8},{8,0},{1,9},{9,1},{2,10},{10,2},{3,11},{11,3},{4,12},{12,4},... | collective-permute-start | bytes 1572872 | tf_op jit(solution)/shard_map/ppermute | solution.py:42
  281.4 41.0 %collective-permute-start.37 = (bf16[8,64,1024]{2,1,0:T(8,128)(2,1)}, bf16[8,64,1024]{2,1,0:T(8,128)(2,1)}, u32[]{:S(2)}, u32[]{:S(2)}) collective-permute-start(bf16[8,64,1024]{2,1,0:T(8,128)(2,1)} %get-tuple-element.74), channel_id=1, source_target_pairs={{0,2},{2,0},{1,3},{3,1},{4,6},{6,4},{5,7},{7,5},{8,10},{10,8},{9,1... | collective-permute-start | bytes 3145736 | tf_op jit(solution)/shard_map/ppermute | solution.py:42
  311.1 56.4 %collective-permute-start.25 = (bf16[256,1024]{1,0:T(8,128)(2,1)}, bf16[256,1024]{1,0:T(8,128)(2,1)}, u32[]{:S(2)}, u32[]{:S(2)}) collective-permute-start(bf16[256,1024]{1,0:T(8,128)(2,1)} %get-tuple-element.118), channel_id=1, source_target_pairs={{0,2},{2,0},{1,3},{3,1},{4,6},{6,4},{5,7},{7,5},{8,10},{10,8},{9,1... | collective-permute-start | bytes 1572872 | tf_op jit(solution)/shard_map/ppermute | solution.py:42
  311.6 12.7 %collective-permute-start.26 = (bf16[256,1024]{1,0:T(8,128)(2,1)}, bf16[256,1024]{1,0:T(8,128)(2,1)}, u32[]{:S(2)}, u32[]{:S(2)}) collective-permute-start(bf16[256,1024]{1,0:T(8,128)(2,1)} %get-tuple-element.117), channel_id=1, source_target_pairs={{0,2},{2,0},{1,3},{3,1},{4,6},{6,4},{5,7},{7,5},{8,10},{10,8},{9,1... | collective-permute-start | bytes 1572872 | tf_op jit(solution)/shard_map/ppermute | solution.py:42
  321.1 60.4 %collective-permute-start.29 = (bf16[8,128,1024]{2,1,0:T(8,128)(2,1)}, bf16[8,128,1024]{2,1,0:T(8,128)(2,1)}, u32[]{:S(2)}, u32[]{:S(2)}) collective-permute-start(bf16[8,128,1024]{2,1,0:T(8,128)(2,1)} %get-tuple-element.69), channel_id=1, source_target_pairs={{0,2},{2,0},{1,3},{3,1},{4,6},{6,4},{5,7},{7,5},{8,10},{10,8},{9,1... | collective-permute-start | bytes 6291464 | tf_op jit(solution)/shard_map/ppermute | solution.py:42
  324.2 11.1 %collective-permute-start.40 = (bf16[2,2,64,512]{3,2,0,1:T(8,128)(2,1)S(1)}, bf16[2,2,64,512]{3,2,0,1:T(8,128)(2,1)S(1)}, u32[]{:S(2)}, u32[]{:S(2)}) collective-permute-start(bf16[2,2,64,512]{3,2,0,1:T(8,128)(2,1)S(1)} %broadcast_select_fusion.3), channel_id=1, source_target_pairs={{0,1},{1,0},{2,3},{3,2},{4,5},{5,4},{6,7},{7,6},{8,9},{9,8},{10,11... | collective-permute-start | bytes 786440 | tf_op jit(solution)/shard_map/ppermute | solution.py:42
  327.0 40.5 %collective-permute-start.27 = (bf16[256,1024]{1,0:T(8,128)(2,1)S(1)}, bf16[256,1024]{1,0:T(8,128)(2,1)S(1)}, u32[]{:S(2)}, u32[]{:S(2)}) collective-permute-start(bf16[256,1024]{1,0:T(8,128)(2,1)S(1)} %add_convert_fusion.3), channel_id=1, source_target_pairs={{0,4},{4,0},{1,5},{5,1},{2,6},{6,2},{3,7},{7,3},{8,12},{12,8},{9,1... | collective-permute-start | bytes 1572872 | tf_op jit(solution)/shard_map/ppermute | solution.py:42
  335.4 20.6 %collective-permute-start.38 = (bf16[2,64,1024]{2,1,0:T(8,128)(2,1)S(1)}, bf16[2,64,1024]{2,1,0:T(8,128)(2,1)S(1)}, u32[]{:S(2)}, u32[]{:S(2)}) collective-permute-start(bf16[2,64,1024]{2,1,0:T(8,128)(2,1)S(1)} %dynamic-slice_bitcast_fusion.1), channel_id=1, source_target_pairs={{0,4},{4,0},{1,5},{5,1},{2,6},{6,2},{3,7},{7,3},{8,12},{12,8},{9,1... | collective-permute-start | bytes 786440 | tf_op jit(solution)/shard_map/ppermute | solution.py:42
  367.5 9.9 %collective-permute-start.43 = (bf16[64,512]{1,0:T(8,128)(2,1)S(1)}, bf16[64,512]{1,0:T(8,128)(2,1)S(1)}, u32[]{:S(2)}, u32[]{:S(2)}) collective-permute-start(bf16[64,512]{1,0:T(8,128)(2,1)S(1)} %get-tuple-element.151), channel_id=1, source_target_pairs={{0,16},{8,24},{16,0},{24,8},{1,17},{9,25},{17,1},{25,9},{2,18},{10... | collective-permute-start | bytes 196616 | tf_op jit(solution)/shard_map/ppermute | solution.py:323
  367.5 9.9 %collective-permute-start.44 = (bf16[64,512]{1,0:T(8,128)(2,1)S(1)}, bf16[64,512]{1,0:T(8,128)(2,1)S(1)}, u32[]{:S(2)}, u32[]{:S(2)}) collective-permute-start(bf16[64,512]{1,0:T(8,128)(2,1)S(1)} %get-tuple-element.148), channel_id=1, source_target_pairs={{0,24},{8,0},{16,8},{24,16},{1,25},{9,1},{17,9},{25,17},{2,26},{10... | collective-permute-start | bytes 196616 | tf_op jit(solution)/shard_map/ppermute | solution.py:323
  374.5 16.0 %collective-permute-start.28 = (bf16[256,1024]{1,0:T(8,128)(2,1)}, bf16[256,1024]{1,0:T(8,128)(2,1)}, u32[]{:S(2)}, u32[]{:S(2)}) collective-permute-start(bf16[256,1024]{1,0:T(8,128)(2,1)} %fusion.19), channel_id=1, source_target_pairs={{8,0},{16,8},{24,16},{9,1},{17,9},{25,17},{10,2},{18,10},{26,18},{... | collective-permute-start | bytes 1572872 | tf_op jit(solution)/shard_map/ppermute | solution.py:76
  385.1 14.0 %collective-permute-start.30 = (bf16[2,128,1024]{2,1,0:T(8,128)(2,1)S(1)}, bf16[2,128,1024]{2,1,0:T(8,128)(2,1)S(1)}, u32[]{:S(2)}, u32[]{:S(2)}) collective-permute-start(bf16[2,128,1024]{2,1,0:T(8,128)(2,1)S(1)} %dynamic-slice_bitcast_fusion), channel_id=1, source_target_pairs={{0,4},{4,0},{1,5},{5,1},{2,6},{6,2},{3,7},{7,3},{8,12},{12,8},{9,1... | collective-permute-start | bytes 1572872 | tf_op jit(solution)/shard_map/ppermute | solution.py:42
  386.9 13.7 %collective-permute-start.32 = (bf16[2,2,128,512]{3,2,0,1:T(8,128)(2,1)S(1)}, bf16[2,2,128,512]{3,2,0,1:T(8,128)(2,1)S(1)}, u32[]{:S(2)}, u32[]{:S(2)}) collective-permute-start(bf16[2,2,128,512]{3,2,0,1:T(8,128)(2,1)S(1)} %broadcast_select_fusion.2), channel_id=1, source_target_pairs={{0,1},{1,0},{2,3},{3,2},{4,5},{5,4},{6,7},{7,6},{8,9},{9,8},{10,11... | collective-permute-start | bytes 1572872 | tf_op jit(solution)/shard_map/ppermute | solution.py:42
  399.3 7.5 %collective-permute-start.31 = (bf16[2,128,512]{2,1,0:T(8,128)(2,1)S(1)}, bf16[2,128,512]{2,1,0:T(8,128)(2,1)S(1)}, u32[]{:S(2)}, u32[]{:S(2)}) collective-permute-start(bf16[2,128,512]{2,1,0:T(8,128)(2,1)S(1)} %broadcast_select_fusion.4), channel_id=1, source_target_pairs={{0,1},{1,0},{2,3},{3,2},{4,5},{5,4},{6,7},{7,6},{8,9},{9,8},{10,11... | collective-permute-start | bytes 786440 | tf_op jit(solution)/shard_map/ppermute | solution.py:42
  401.5 7.5 %collective-permute-start.33 = (bf16[2,128,512]{2,1,0:T(8,128)(2,1)}, bf16[2,128,512]{2,1,0:T(8,128)(2,1)}, u32[]{:S(2)}, u32[]{:S(2)}) collective-permute-start(bf16[2,128,512]{2,1,0:T(8,128)(2,1)} %dynamic-slice_bitcast_fusion.2), channel_id=1, source_target_pairs={{0,4},{4,0},{1,5},{5,1},{2,6},{6,2},{3,7},{7,3},{8,12},{12,8},{9,1... | collective-permute-start | bytes 786440 | tf_op jit(solution)/shard_map/ppermute | solution.py:42
  408.6 8.2 %collective-permute-start.45 = (bf16[64,2,576]{2,0,1:T(8,128)(2,1)S(1)}, bf16[64,2,576]{2,0,1:T(8,128)(2,1)S(1)}, u32[]{:S(2)}, u32[]{:S(2)}) collective-permute-start(bf16[64,2,576]{2,0,1:T(8,128)(2,1)S(1)} %bitcast.296), channel_id=1, source_target_pairs={{0,2},{2,0},{1,3},{3,1},{4,6},{6,4},{5,7},{7,5},{8,10},{10,8},{9,1... | collective-permute-start | bytes 442376 | tf_op jit(solution)/shard_map/ppermute | solution.py:42
  411.1 10.9 %collective-permute-start.34 = (bf16[128,512]{1,0:T(8,128)(2,1)}, bf16[128,512]{1,0:T(8,128)(2,1)S(1)}, u32[]{:S(2)}, u32[]{:S(2)}) collective-permute-start(bf16[128,512]{1,0:T(8,128)(2,1)} %get-tuple-element.138), channel_id=1, source_target_pairs={{0,8},{8,16},{16,24},{24,0},{1,9},{9,17},{17,25},{25,1},{2,10},{10... | collective-permute-start | bytes 393224 | tf_op jit(solution)/shard_map/ppermute | solution.py:323
  414.4 9.9 %collective-permute-start.35 = (bf16[128,512]{1,0:T(8,128)(2,1)}, bf16[128,512]{1,0:T(8,128)(2,1)S(1)}, u32[]{:S(2)}, u32[]{:S(2)}) collective-permute-start(bf16[128,512]{1,0:T(8,128)(2,1)} %get-tuple-element.139), channel_id=1, source_target_pairs={{0,16},{8,24},{16,0},{24,8},{1,17},{9,25},{17,1},{25,9},{2,18},{10... | collective-permute-start | bytes 393224 | tf_op jit(solution)/shard_map/ppermute | solution.py:323
  414.4 10.2 %collective-permute-start.36 = (bf16[128,512]{1,0:T(8,128)(2,1)}, bf16[128,512]{1,0:T(8,128)(2,1)}, u32[]{:S(2)}, u32[]{:S(2)}) collective-permute-start(bf16[128,512]{1,0:T(8,128)(2,1)} %get-tuple-element.136), channel_id=1, source_target_pairs={{0,24},{8,0},{16,8},{24,16},{1,25},{9,1},{17,9},{25,17},{2,26},{10... | collective-permute-start | bytes 393224 | tf_op jit(solution)/shard_map/ppermute | solution.py:323
  417.5 11.3 %collective-permute-start.46 = (bf16[64,2304]{1,0:T(8,128)(2,1)S(1)}, bf16[64,2304]{1,0:T(8,128)(2,1)S(1)}, u32[]{:S(2)}, u32[]{:S(2)}) collective-permute-start(bf16[64,2304]{1,0:T(8,128)(2,1)S(1)} %reshape.388), channel_id=1, source_target_pairs={{0,0},{1,8},{8,1},{9,9},{2,2},{3,10},{10,3},{11,11},{4,4},{5,12},{... | collective-permute-start | bytes 884744 | tf_op jit(solution)/shard_map/ppermute | solution.py:484
  (69 other events, 558.9 us)
Sparse Core Ops, SparseCore 0:
  10.9 101.9 all-gather.5
  115.6 55.7 all-gather.3
  228.0 55.7 reduce-scatter.4
  287.7 94.9 reduce-scatter.2
